TPU v7x, 32 devices: a whole 2x2x4 slice. The times are simulated.
32 devices in a mesh: wide: 4 (over y, core), blk: 8 (over z, x).
Axes of the slice: x: 2, y: 2, z: 4, core: 2. Of those that a mesh axis runs over, the one named last changes fastest.
Arguments:
- flux_rows: float32 [32768, 1024], P(('wide', 'blk')), may hold values from -36 to 36
- row_signs: int32 [32768], P(('wide', 'blk')), may hold values from -1 to 1, as said below
- sample_rows: int32 [65536], P(('wide', 'blk')), may hold values from 0 to 1023
- sample_owner: int32 [65536, 1], P(('wide', 'blk')), may hold values from 0 to 7; in each aligned block of 2048 rows (0 to 2047, 2048 to 4095, ...) at most 640 rows name the same one
Outputs:
- transformed: bfloat16 [32768, 1024], P(('wide', 'blk'))
- sketch_factors: float32 [8192, 1024], P(('wide', 'blk'))
Inputs may be any that keep to these rules, and one draw needn't show every extreme that they name: `row_signs`: every entry is -1 or 1. `sample_owner`: among the 2048 sampled rows of one device, no owner is named by more than 640 rows, a bound that some block reaches.
All inputs are finite; a program needn't handle non-finite values.
Results may differ from a plain program's by a relative error of at most 0.0058.
Values may be sent and summed in bfloat16 or wider, within the bound.
No kernel may reach another device: no remote copies, remote signals or barrier semaphores. Data moves between devices by JAX's collectives and lax.ppermute only.
A program may use at most 128 MiB of HBM per device.

v0:
```python
import functools

import jax
import jax.numpy as jnp
import numpy as np
from jax import lax
from jax.experimental import pallas as pl
from jax.experimental.pallas import tpu as pltpu
from jax.sharding import PartitionSpec as P

PANEL = 256
HB = 128
NZ = 4
CHUNKS = ((0, 256), (256, 256), (512, 256), (768, 256))
SQRT_HALF = 0.7071067811865476
HIGHEST = lax.Precision.HIGHEST
F32 = jnp.float32
BF16 = jnp.bfloat16


def hadamard_pair():
    idx = np.arange(HB)
    common = idx[:, None] & idx[None, :]
    parity = np.zeros_like(common)
    for bit in range(HB.bit_length() - 1):
        parity ^= (common >> bit) & 1
    one = 1.0 - 2.0 * parity
    return jnp.asarray(np.kron(np.eye(2), one), BF16)


VMEM_LIMIT = 24 << 20


def params(**kw):
    return pltpu.CompilerParams(vmem_limit_bytes=VMEM_LIMIT, **kw)


def cost(flops, moved):
    return pl.CostEstimate(flops=flops, bytes_accessed=moved, transcendentals=0)


def mix_kernel(signs_ref, had_ref, x_ref, out_ref):
    signed = (had_ref[...].astype(F32) * signs_ref[...].astype(F32)).astype(BF16)
    x = x_ref[...]
    hi = x.astype(BF16)
    rest = x - hi.astype(F32)
    mid = rest.astype(BF16)
    low = (rest - mid.astype(F32)).astype(BF16)
    total = jnp.dot(signed, low, preferred_element_type=F32)
    total = total + jnp.dot(signed, mid, preferred_element_type=F32)
    total = total + jnp.dot(signed, hi, preferred_element_type=F32)
    out_ref[...] = (total * (HB**-0.5)).astype(BF16)


def mix_chunk(signs, had, flux, start, width):
    rows = flux.shape[0]
    size = had.shape[0]
    block = start // width
    return pl.pallas_call(
        mix_kernel,
        grid=(rows // size,),
        in_specs=[
            pl.BlockSpec((1, size), lambda i: (0, i)),
            pl.BlockSpec(had.shape, lambda i: (0, 0)),
            pl.BlockSpec((size, width), lambda i: (i, block)),
        ],
        out_specs=pl.BlockSpec((size, width), lambda i: (i, 0)),
        out_shape=jax.ShapeDtypeStruct((rows, width), BF16),
        cost_estimate=cost(2 * rows * width * size * 3, rows * width * 6),
        name="mix",
    )(signs, had, flux)


def join_kernel(sign_ref, own_ref, other_ref, *refs):
    total = (other_ref[...].astype(F32) + own_ref[...].astype(F32) * sign_ref[0]) * SQRT_HALF
    total = total.astype(BF16)
    for ref in refs[-2:]:
        ref[...] = total


def join_last(own, other, sign, start, columns, whole):
    rows, width = own.shape
    block = start // width
    tile = rows // 2
    chunk = pl.BlockSpec((tile, width), lambda i: (i, 0))
    operands, specs, alias = [sign.reshape(1), own, other], [pl.BlockSpec(memory_space=pltpu.SMEM), chunk, chunk], {}
    if whole is not None:
        operands.append(whole)
        specs.append(pl.BlockSpec(memory_space=pl.ANY))
        alias = {3: 1}
    return pl.pallas_call(
        join_kernel,
        grid=(rows // tile,),
        in_specs=specs,
        out_specs=(chunk, pl.BlockSpec((tile, width), lambda i: (i, block))),
        out_shape=(jax.ShapeDtypeStruct((rows, width), BF16), jax.ShapeDtypeStruct((rows, columns), BF16)),
        input_output_aliases=alias,
        compiler_params=params(),
        cost_estimate=cost(4 * rows * width, 8 * rows * width),
        name="join",
    )(*operands)


def relative_owner(q):
    return ((q & 1) << 1) | (q >> 1)


def count_kernel(nx, me_ref, rows_ref, owner_ref, *out_refs):
    listed = rows_ref.shape[1]
    rows = out_refs[0].shape[1]
    me_z, me_x = me_ref[0], me_ref[1]
    index = lax.broadcasted_iota(jnp.int32, (NZ * nx, listed), 0)
    q, s = index & (NZ - 1), index >> (NZ.bit_length() - 1)
    z = me_z ^ relative_owner(q)
    x = (me_x + s) & (nx - 1)
    by_owner = (z * nx + x == owner_ref[...]).astype(F32).astype(BF16)
    by_row = (lax.broadcasted_iota(jnp.int32, (rows, listed), 0) == rows_ref[...]).astype(F32).astype(BF16)
    total = lax.dot_general(by_owner, by_row, (((1,), (1,)), ((), ())), preferred_element_type=F32)
    for shift, ref in enumerate(out_refs):
        ref[...] = total[shift * NZ : (shift + 1) * NZ, :]


def count_samples(sample_rows, sample_owner, nx, rows, me_z, me_x):
    listed = sample_rows.shape[0]
    shape = jax.ShapeDtypeStruct((NZ, rows), F32)
    vmem = pl.BlockSpec(memory_space=pltpu.VMEM)
    return pl.pallas_call(
        functools.partial(count_kernel, nx),
        in_specs=[pl.BlockSpec(memory_space=pltpu.SMEM), vmem, vmem],
        out_shape=(shape,) * nx,
        compiler_params=params(),
        cost_estimate=cost(2 * rows * listed * NZ * nx, rows * NZ * nx * 4),
        name="counts",
    )(jnp.stack([me_z, me_x]), sample_rows.reshape(1, listed), sample_owner.reshape(1, listed))


def weigh_kernel(counts_ref, lead_ref, hi_ref, lo_ref):
    lead = lead_ref[...].astype(F32).T
    for q in range(NZ):
        part = pl.ds(q * PANEL, PANEL)
        weighed = lead * counts_ref[q : q + 1, :]
        hi = weighed.astype(BF16)
        hi_ref[part, :] = hi
        lo_ref[part, :] = (weighed - hi.astype(F32)).astype(BF16)


def weigh(counts, lead):
    rows = lead.shape[0]
    tile = rows // 2
    out = pl.BlockSpec((NZ * PANEL, tile), lambda i: (0, i))
    shape = jax.ShapeDtypeStruct((NZ * PANEL, rows), BF16)
    return pl.pallas_call(
        weigh_kernel,
        grid=(rows // tile,),
        in_specs=[pl.BlockSpec((NZ, tile), lambda i: (0, i)), pl.BlockSpec((tile, PANEL), lambda i: (i, 0))],
        out_specs=(out, out),
        out_shape=(shape, shape),
        compiler_params=params(),
        cost_estimate=cost(rows * PANEL * 16, rows * PANEL * 18),
        name="weigh",
    )(counts, lead)


GRAM_TILES = 2


def gram_kernel(parts, packed, *refs):
    keep_ref, send_ref, acc = refs[-3:]
    step = pl.program_id(0)

    @pl.when(step == 0)
    def _():
        acc[...] = jnp.zeros_like(acc)

    for p in range(parts):
        hi_ref, lo_ref, rows_ref = refs[3 * p : 3 * p + 3]

        @pl.when(step // GRAM_TILES == p)
        def _(hi_ref=hi_ref, lo_ref=lo_ref, rows_ref=rows_ref):
            rows = rows_ref[...]
            low = jnp.dot(lo_ref[...], rows, preferred_element_type=F32)
            acc[...] += low + jnp.dot(hi_ref[...], rows, preferred_element_type=F32)

    @pl.when(step == parts * GRAM_TILES - 1)
    def _():
        half = PANEL // 2
        for q in range(NZ):
            ref, place = (keep_ref, q) if q < NZ // 2 else (send_ref, q - NZ // 2)
            base = q * PANEL
            if packed:
                to = place * 3 * half
                ref[to : to + PANEL, :] = acc[base : base + PANEL, :half]
                ref[to + PANEL : to + 3 * half, :] = acc[base + half : base + PANEL, half:]
            else:
                ref[place * PANEL : (place + 1) * PANEL, :] = acc[base : base + PANEL, :]


def partial_grams(weights, chunk_rows, packed):
    parts = len(chunk_rows)
    rows, width = chunk_rows[0].shape
    tile = rows // GRAM_TILES
    half = NZ // 2
    shape = (half * (PANEL + PANEL // 2), PANEL // 2) if packed else (half * PANEL, width)
    operands, specs = [], []
    for p, ((hi, lo), block) in enumerate(zip(weights, chunk_rows)):
        operands += [hi, lo, block]

        def place(k, p=p):
            return jnp.clip(k - p * GRAM_TILES, 0, GRAM_TILES - 1)

        weight_spec = pl.BlockSpec((NZ * PANEL, tile), lambda k, place=place: (0, place(k)))
        specs += [weight_spec, weight_spec, pl.BlockSpec((tile, width), lambda k, place=place: (place(k), 0))]
    out = pl.BlockSpec(shape, lambda k: (0, 0))
    out_shape = jax.ShapeDtypeStruct(shape, F32)
    return pl.pallas_call(
        functools.partial(gram_kernel, parts, packed),
        grid=(parts * GRAM_TILES,),
        in_specs=specs,
        out_specs=(out, out),
        out_shape=(out_shape, out_shape),
        scratch_shapes=[pltpu.VMEM((NZ * PANEL, width), F32)],
        compiler_params=params(),
        cost_estimate=cost(4 * parts * NZ * PANEL * rows * width, 4 * parts * NZ * PANEL * rows + 2 * parts * rows * width),
        name="grams",
    )(*operands)


def add_kernel(keep_ref, near_ref, out_ref):
    out_ref[...] = keep_ref[...] + near_ref[...]


def far_sum(keep, near):
    rows, width = keep.shape[0] // 2, keep.shape[1]
    spec = pl.BlockSpec((rows, width), lambda i: (1, 0))
    return pl.pallas_call(
        add_kernel,
        grid=(1,),
        in_specs=[spec, spec],
        out_specs=pl.BlockSpec((rows, width), lambda i: (0, 0)),
        out_shape=jax.ShapeDtypeStruct((rows, width), F32),
        compiler_params=params(),
        cost_estimate=cost(rows * width, 12 * rows * width),
        name="add",
    )(keep, near)


BAND = 32
CUT = 4


def eliminate(work, first, last):
    rb = lax.broadcasted_iota(jnp.int32, (BAND, BAND), 0)
    cb = lax.broadcasted_iota(jnp.int32, (BAND, BAND), 1)
    eye_b = (rb == cb).astype(F32)
    row_id = lax.broadcasted_iota(jnp.int32, (BAND, 1), 0)
    for k in range(first, last):
        lo, hi = k * BAND, (k + 1) * BAND
        tile = jnp.concatenate([work[lo:hi, lo:hi], eye_b], axis=1)
        for j in range(BAND):
            pivot = tile[j : j + 1, j : j + 1]
            r = lax.rsqrt(pivot)
            r = r * (1.5 - 0.5 * pivot * r * r)
            row = tile[j : j + 1, :] * r
            column = tile[:, j : j + 1] * r
            tile = jnp.where(row_id == j, row, jnp.where(row_id > j, tile - column * row, tile))
        inv = jnp.where(rb >= cb, tile[:, BAND:], 0.0)
        full = jnp.dot(inv, work[lo:hi, lo:], precision=HIGHEST, preferred_element_type=F32)
        if hi < PANEL:
            panel = full[:, BAND : PANEL - lo]
            work[hi:, hi:] = work[hi:, hi:] - lax.dot_general(
                panel, full[:, BAND:], (((0,), (0,)), ((), ())), precision=HIGHEST, preferred_element_type=F32
            )
        work[lo:hi, lo:] = full


def factor_first_kernel(scale, keep_ref, near_ref, far_ref, out_ref, work):
    half = PANEL // 2
    lead = (keep_ref[...] + near_ref[...] + far_ref[...]) * scale
    ri = lax.broadcasted_iota(jnp.int32, (PANEL, PANEL), 0)
    ci = lax.broadcasted_iota(jnp.int32, (PANEL, PANEL), 1)
    eye = (ri == ci).astype(F32)
    work[:, PANEL:] = eye
    work[:half, :half] = lead[:half, :] + 0.5 * eye[:half, :half]
    work[:half, half:PANEL] = lead[half:PANEL, :].T
    work[half:, :half] = lead[half:PANEL, :]
    work[half:, half:PANEL] = lead[PANEL:, :] + 0.5 * eye[:half, :half]
    eliminate(work, 0, CUT)
    out_ref[...] = work[...]


def factor_last_kernel(in_ref, out_ref, inverse_ref, work):
    work[...] = in_ref[...]
    eliminate(work, CUT, PANEL // BAND)
    ri = lax.broadcasted_iota(jnp.int32, (PANEL, PANEL), 0)
    ci = lax.broadcasted_iota(jnp.int32, (PANEL, PANEL), 1)
    out_ref[...] = jnp.where(ci >= ri, work[:, :PANEL], 0.0)
    inverse_ref[...] = jnp.where(ri >= ci, work[:, PANEL:], 0.0)


def factor_first(keep, near, far, scale):
    spec = pl.BlockSpec(far.shape, lambda i: (0, 0))
    shape = (PANEL, 2 * PANEL)
    return pl.pallas_call(
        functools.partial(factor_first_kernel, scale),
        grid=(1,),
        in_specs=[spec, spec, spec],
        out_specs=pl.BlockSpec(shape, lambda i: (0, 0)),
        out_shape=jax.ShapeDtypeStruct(shape, F32),
        scratch_shapes=[pltpu.VMEM(shape, F32)],
        compiler_params=params(),
        cost_estimate=cost(10_000_000_000, 1 << 20),
        name="factor_first",
    )(keep, near, far)


def factor_last(state, columns):
    square = pl.BlockSpec((PANEL, PANEL), lambda i: (0, 0))
    return pl.pallas_call(
        factor_last_kernel,
        grid=(1,),
        in_specs=[pl.BlockSpec(state.shape, lambda i: (0, 0))],
        out_specs=(square, square),
        out_shape=(jax.ShapeDtypeStruct((PANEL, columns), F32), jax.ShapeDtypeStruct((PANEL, PANEL), F32)),
        scratch_shapes=[pltpu.VMEM(state.shape, F32)],
        compiler_params=params(),
        cost_estimate=cost(10_000_000_000, 1 << 20),
        name="factor_last",
    )(state)


def couple_kernel(scale, inverse_ref, keep_ref, near_ref, far_ref, whole_ref, out_ref):
    gram = (keep_ref[...] + near_ref[...] + far_ref[...]) * scale
    out_ref[...] = jnp.dot(inverse_ref[...], gram, precision=HIGHEST, preferred_element_type=F32)


def couple(inverse, keep, near, far, whole, start, scale):
    rows, width = far.shape
    block = start // width
    spec = pl.BlockSpec((rows, width), lambda i: (0, 0))
    return pl.pallas_call(
        functools.partial(couple_kernel, scale),
        grid=(1,),
        in_specs=[pl.BlockSpec(inverse.shape, lambda i: (0, 0)), spec, spec, spec, pl.BlockSpec(memory_space=pl.ANY)],
        out_specs=pl.BlockSpec((rows, width), lambda i: (0, block)),
        out_shape=jax.ShapeDtypeStruct(whole.shape, F32),
        input_output_aliases={4: 0},
        compiler_params=params(),
        cost_estimate=cost(12 * PANEL * rows * width, 20 * rows * width),
        name="couple",
    )(inverse, keep, near, far, whole)


def per_device(flux_rows, row_signs, sample_rows, sample_owner):
    wide, blk = lax.axis_size("wide"), lax.axis_size("blk")
    nx = blk // NZ
    rows, columns = flux_rows.shape
    scale = 1.0 / sample_rows.shape[0]
    me_w, me_b = lax.axis_index("wide"), lax.axis_index("blk")
    me_x, me_z = me_b & (nx - 1), me_b >> (nx.bit_length() - 1)
    had = hadamard_pair()
    signs = row_signs.reshape(1, rows)
    levels = wide.bit_length() - 1

    def at(z, x):
        return z * nx + x

    def z_route(mask):
        return [(at(z, x), at(z ^ mask, x)) for z in range(NZ) for x in range(nx)]

    def x_shift(s):
        return [(at(z, x), at(z, (x + s) % nx)) for z in range(NZ) for x in range(nx)]

    def level_sign(level):
        return jnp.where((me_w >> level) & 1 == 1, -1.0, 1.0).astype(F32)

    chunks = range(len(CHUNKS))
    current = []
    for i in chunks:
        start, width = CHUNKS[i]
        current.append(mix_chunk(signs, had, flux_rows, start, width))
    for level in range(levels - 1):
        for i in chunks:
            partner = lax.ppermute(current[i], "wide", [(w, w ^ (1 << level)) for w in range(wide)])
            own = current[i].astype(F32)
            current[i] = ((partner.astype(F32) + own * level_sign(level)) * SQRT_HALF).astype(BF16)

    counts = count_samples(sample_rows, sample_owner, nx, rows, me_z, me_x)
    owner_counts = [counts[0]]
    for s in range(1, nx):
        owner_counts.append(lax.ppermute(counts[s], "blk", x_shift(s)))

    whole, sources = None, []
    for i in chunks:
        start, width = CHUNKS[i]
        partner = lax.ppermute(current[i], "wide", [(w, w ^ (wide // 2)) for w in range(wide)])
        current[i], whole = join_last(current[i], partner, level_sign(levels - 1), start, columns, whole)
        sources.append([current[i]])
        for s in range(1, nx):
            sources[i].append(lax.ppermute(current[i], "blk", x_shift(s)))

    weights, grams = [], []
    for p in range(nx):
        weights.append(weigh(owner_counts[p], sources[0][p]))
    for i in chunks:
        keep, send = partial_grams(weights, sources[i], i == 0)
        near = lax.ppermute(send, "blk", z_route(1))
        onward = far_sum(keep, near)
        far = lax.ppermute(onward, "blk", z_route(2))
        grams.append((keep, near, far))
    state = factor_first(*grams[0], scale)
    sketch, inverse = factor_last(state, columns)
    for i in chunks[1:]:
        sketch = couple(inverse, *grams[i], sketch, CHUNKS[i][0], scale)
    return whole, sketch


def solution(mesh):
    placed = (
        P(("wide", "blk"), None),
        P(("wide", "blk")),
        P(("wide", "blk")),
        P(("wide", "blk"), None),
    )

    return jax.shard_map(
        per_device,
        mesh=mesh,
        in_specs=placed,
        out_specs=(P(("wide", "blk"), None), P(("wide", "blk"), None)),
        check_vma=False,
    )
```

profile of v0, /device:TPU:0, one launch (start us, length us, event | category | flops | bytes accessed | tf_op | source)
XLA Modules:
  0.0 180.5 jit_solution(4199790091363620167)
XLA Ops:
  0.6 3.9 %mix.5 = bf16[1024,256]{1,0:T(8,128)(2,1)} custom-call(s32[1,1024]{1,0:T(1,128)} %bitcast.8, bf16[256,256]{1,0:T(8,128)(2,1)} %constant.20.clone.had_ref, f32[1024,1024]{1,0:T(8,128)} %x_ref.7), custom_call_target="tpu_custom_call" | custom-call | flops 402653184 | bytes 1572864 | tf_op jit(solution)/shard_map/mix/pallas_call | solution.py:59
  4.5 0.5 collective-permute-start.2
  5.0 3.9 %mix.7 = bf16[1024,256]{1,0:T(8,128)(2,1)} custom-call(s32[1,1024]{1,0:T(1,128)} %bitcast.9, bf16[256,256]{1,0:T(8,128)(2,1)} %constant.20.clone.had_ref, f32[1024,1024]{1,0:T(8,128)} %x_ref.7), custom_call_target="tpu_custom_call" | custom-call | flops 402653184 | bytes 1572864 | tf_op jit(solution)/shard_map/mix/pallas_call | solution.py:59
  8.9 3.9 %mix.4 = bf16[1024,256]{1,0:T(8,128)(2,1)} custom-call(s32[1,1024]{1,0:T(1,128)} %bitcast.10, bf16[256,256]{1,0:T(8,128)(2,1)} %constant.20.clone.had_ref, f32[1024,1024]{1,0:T(8,128)} %x_ref.7), custom_call_target="tpu_custom_call" | custom-call | flops 402653184 | bytes 1572864 | tf_op jit(solution)/shard_map/mix/pallas_call | solution.py:59
  12.8 0.5 collective-permute-start
  13.3 3.9 %mix.6 = bf16[1024,256]{1,0:T(8,128)(2,1)} custom-call(s32[1,1024]{1,0:T(1,128)} %bitcast.11, bf16[256,256]{1,0:T(8,128)(2,1)} %constant.20.clone.had_ref, f32[1024,1024]{1,0:T(8,128)} %x_ref.7), custom_call_target="tpu_custom_call" | custom-call | flops 402653184 | bytes 1572864 | tf_op jit(solution)/shard_map/mix/pallas_call | solution.py:59
  17.3 1.3 multiply_convert_fusion.2.own_ref
  18.6 3.0 %collective-permute-start.3 = (bf16[1024,256]{1,0:T(8,128)(2,1)S(1)}, bf16[1024,256]{1,0:T(8,128)(2,1)}, u32[]{:S(2)}, u32[]{:S(2)}) collective-permute-start(bf16[1024,256]{1,0:T(8,128)(2,1)S(1)} %multiply_convert_fusion.2.own_ref), channel_id=1, source_target_pairs={{0,16},{8,24},{16,0},{24,8},{1,17},{9,25},{17,1},{25,9},{2,18},{10... | collective-permute-start | bytes 1572872 | tf_op jit(solution)/shard_map/ppermute | solution.py:395
  21.5 0.2 multiply_convert_fusion.own_ref
  21.8 1.2 multiply_convert_fusion.1.own_ref
  23.1 2.1 %collective-permute-start.5 = (bf16[1024,256]{1,0:T(8,128)(2,1)S(1)}, bf16[1024,256]{1,0:T(8,128)(2,1)}, u32[]{:S(2)}, u32[]{:S(2)}) collective-permute-start(bf16[1024,256]{1,0:T(8,128)(2,1)S(1)} %multiply_convert_fusion.1.own_ref), channel_id=1, source_target_pairs={{0,16},{8,24},{16,0},{24,8},{1,17},{9,25},{17,1},{25,9},{2,18},{10... | collective-permute-start | bytes 1572872 | tf_op jit(solution)/shard_map/ppermute | solution.py:395
  25.1 1.2 multiply_convert_fusion.3.own_ref
  26.5 19.1 %collective-permute-done.7.other_ref = bf16[1024,256]{1,0:T(8,128)(2,1)S(1)} collective-permute-done((bf16[1024,256]{1,0:T(8,128)(2,1)S(1)}, bf16[1024,256]{1,0:T(8,128)(2,1)S(1)}, u32[]{:S(2)}, u32[]{:S(2)}) %collective-permute-start.7) | collective-permute-done | bytes 524320 | tf_op jit(solution)/shard_map/ppermute | solution.py:395
  45.5 0.9 join.4
  46.5 2.0 %collective-permute-start.9 = (bf16[1024,256]{1,0:T(8,128)(2,1)S(1)}, bf16[1024,256]{1,0:T(8,128)(2,1)S(1)}, u32[]{:S(2)}, u32[]{:S(2)}) collective-permute-start(bf16[1024,256]{1,0:T(8,128)(2,1)S(1)} %get-tuple-element.31.lead_ref.refs_2_), channel_id=1, source_target_pairs={{0,1},{1,0},{2,3},{3,2},{4,5},{5,4},{6,7},{7,6},{8,9},{9,8},{10,11... | collective-permute-start | bytes 1572872 | tf_op jit(solution)/shard_map/ppermute | solution.py:399
  48.5 8.4 %collective-permute-done.5.other_ref = bf16[1024,256]{1,0:T(8,128)(2,1)} collective-permute-done((bf16[1024,256]{1,0:T(8,128)(2,1)S(1)}, bf16[1024,256]{1,0:T(8,128)(2,1)}, u32[]{:S(2)}, u32[]{:S(2)}) %collective-permute-start.5) | collective-permute-done | bytes 524320 | tf_op jit(solution)/shard_map/ppermute | solution.py:395
  56.9 1.9 %join.5 = (bf16[1024,256]{1,0:T(8,128)(2,1)S(1)}, bf16[1024,1024]{1,0:T(8,128)(2,1)}) custom-call(f32[1]{0:T(128)} %bitcast.sign_ref, bf16[1024,256]{1,0:T(8,128)(2,1)S(1)} %multiply_convert_fusion.1.own_ref, bf16[1024,256]{1,0:T(8,128)(2,1)} %collective-permute-done.5.other_ref, ...), custom_call_target="tpu_custom_call", output_to_operand_aliasing={{1}: (3, {})} | custom-call | flops 1048576 | bytes 2097152 | tf_op jit(solution)/shard_map/join/pallas_call | solution.py:91
  58.8 1.9 %join.6 = (bf16[1024,256]{1,0:T(8,128)(2,1)S(1)}, bf16[1024,1024]{1,0:T(8,128)(2,1)}) custom-call(f32[1]{0:T(128)} %bitcast.sign_ref, bf16[1024,256]{1,0:T(8,128)(2,1)S(1)} %multiply_convert_fusion.2.own_ref, bf16[1024,256]{1,0:T(8,128)(2,1)} %collective-permute-done.3.other_ref, ...), custom_call_target="tpu_custom_call", output_to_operand_aliasing={{1}: (3, {})} | custom-call | flops 1048576 | bytes 2097152 | tf_op jit(solution)/shard_map/join/pallas_call | solution.py:91
  60.6 2.0 %collective-permute-start.15 = (bf16[1024,256]{1,0:T(8,128)(2,1)S(1)}, bf16[1024,256]{1,0:T(8,128)(2,1)S(1)}, u32[]{:S(2)}, u32[]{:S(2)}) collective-permute-start(bf16[1024,256]{1,0:T(8,128)(2,1)S(1)} %get-tuple-element.43.refs_2_), channel_id=1, source_target_pairs={{0,1},{1,0},{2,3},{3,2},{4,5},{5,4},{6,7},{7,6},{8,9},{9,8},{10,11... | collective-permute-start | bytes 1572872 | tf_op jit(solution)/shard_map/ppermute | solution.py:399
  62.6 4.9 %collective-permute-done.1.other_ref = bf16[1024,256]{1,0:T(8,128)(2,1)} collective-permute-done((bf16[1024,256]{1,0:T(8,128)(2,1)S(1)}, bf16[1024,256]{1,0:T(8,128)(2,1)}, u32[]{:S(2)}, u32[]{:S(2)}) %collective-permute-start.1) | collective-permute-done | bytes 524320 | tf_op jit(solution)/shard_map/ppermute | solution.py:395
  67.6 1.9 %join.7 = (bf16[1024,256]{1,0:T(8,128)(2,1)S(1)}, bf16[1024,1024]{1,0:T(8,128)(2,1)}) custom-call(f32[1]{0:T(128)} %bitcast.sign_ref, bf16[1024,256]{1,0:T(8,128)(2,1)S(1)} %multiply_convert_fusion.3.own_ref, bf16[1024,256]{1,0:T(8,128)(2,1)} %collective-permute-done.1.other_ref, ...), custom_call_target="tpu_custom_call", output_to_operand_aliasing={{1}: (3, {})} | custom-call | flops 1048576 | bytes 2097152 | tf_op jit(solution)/shard_map/join/pallas_call | solution.py:91
  69.4 1.7 collective-permute-start.12
  71.2 1.7 counts.1
  72.9 0.3 collective-permute-start.8
  73.3 1.7 collective-permute-start.18
  75.0 1.2 weigh.2
  76.2 10.7 %collective-permute-done.8.counts_ref = f32[4,1024]{1,0:T(4,128)S(1)} collective-permute-done((f32[4,1024]{1,0:T(4,128)S(1)}, f32[4,1024]{1,0:T(4,128)S(1)}, u32[]{:S(2)}, u32[]{:S(2)}) %collective-permute-start.8) | collective-permute-done | bytes 16416 | tf_op jit(solution)/shard_map/ppermute | solution.py:390
  86.9 1.2 weigh.3
  88.1 3.7 %grams.4 = (f32[768,128]{1,0:T(8,128)S(1)}, f32[768,128]{1,0:T(8,128)S(1)}) custom-call(bf16[1024,1024]{1,0:T(8,128)(2,1)S(1)} %get-tuple-element.32.refs_0_, bf16[1024,1024]{1,0:T(8,128)(2,1)S(1)} %get-tuple-element.33.refs_1_, bf16[1024,256]{1,0:T(8,128)(2,1)S(1)} %get-tuple-element.31.lead_ref.refs_2_, bf16[1024,1024]{1,0:T(8,128)(2,1)S(1)} %get-tuple-element.35.refs_3_, ...), custom_call_target="tpu_custom_call" | custom-call | flops 2147483648 | bytes 9437184 | tf_op jit(solution)/shard_map/grams/pallas_call | solution.py:215
  91.8 1.6 collective-permute-start.10
  93.4 3.7 %grams.6 = (f32[512,256]{1,0:T(8,128)S(1)}, f32[512,256]{1,0:T(8,128)S(1)}) custom-call(bf16[1024,1024]{1,0:T(8,128)(2,1)S(1)} %get-tuple-element.32.refs_0_, bf16[1024,1024]{1,0:T(8,128)(2,1)S(1)} %get-tuple-element.33.refs_1_, bf16[1024,256]{1,0:T(8,128)(2,1)S(1)} %get-tuple-element.43.refs_2_, bf16[1024,1024]{1,0:T(8,128)(2,1)S(1)} %get-tuple-element.35.refs_3_, ...), custom_call_target="tpu_custom_call" | custom-call | flops 2147483648 | bytes 9437184 | tf_op jit(solution)/shard_map/grams/pallas_call | solution.py:215
  97.1 0.6 collective-permute-start.16
  97.7 3.7 %grams.5 = (f32[512,256]{1,0:T(8,128)S(1)}, f32[512,256]{1,0:T(8,128)S(1)}) custom-call(bf16[1024,1024]{1,0:T(8,128)(2,1)S(1)} %get-tuple-element.32.refs_0_, bf16[1024,1024]{1,0:T(8,128)(2,1)S(1)} %get-tuple-element.33.refs_1_, bf16[1024,256]{1,0:T(8,128)(2,1)S(1)} %get-tuple-element.40.refs_2_, bf16[1024,1024]{1,0:T(8,128)(2,1)S(1)} %get-tuple-element.35.refs_3_, ...), custom_call_target="tpu_custom_call" | custom-call | flops 2147483648 | bytes 9437184 | tf_op jit(solution)/shard_map/grams/pallas_call | solution.py:215
  101.5 1.6 collective-permute-start.13
  103.0 3.9 %grams.7 = (f32[512,256]{1,0:T(8,128)S(1)}, f32[512,256]{1,0:T(8,128)S(1)}) custom-call(bf16[1024,1024]{1,0:T(8,128)(2,1)S(1)} %get-tuple-element.32.refs_0_, bf16[1024,1024]{1,0:T(8,128)(2,1)S(1)} %get-tuple-element.33.refs_1_, bf16[1024,256]{1,0:T(8,128)(2,1)S(1)} %get-tuple-element.46.refs_2_, bf16[1024,1024]{1,0:T(8,128)(2,1)S(1)} %get-tuple-element.35.refs_3_, ...), custom_call_target="tpu_custom_call" | custom-call | flops 2147483648 | bytes 9437184 | tf_op jit(solution)/shard_map/grams/pallas_call | solution.py:215
  107.0 0.6 collective-permute-start.19
  107.6 2.6 %collective-permute-start.11 = (f32[384,128]{1,0:T(8,128)S(1)}, f32[384,128]{1,0:T(8,128)S(1)}, u32[]{:S(2)}, u32[]{:S(2)}) collective-permute-start(f32[384,128]{1,0:T(8,128)S(1)} %add.26), channel_id=1, source_target_pairs={{0,4},{1,5},{2,6},{3,7},{4,0},{5,1},{6,2},{7,3},{8,12},{9,13},{10,... | collective-permute-start | bytes 589832 | tf_op jit(solution)/shard_map/ppermute | solution.py:408
  110.2 11.5 %collective-permute-done.16.near_ref = f32[512,256]{1,0:T(8,128)S(1)} collective-permute-done((f32[512,256]{1,0:T(8,128)S(1)}, f32[512,256]{1,0:T(8,128)S(1)}, u32[]{:S(2)}, u32[]{:S(2)}) %collective-permute-start.16) | collective-permute-done | bytes 524320 | tf_op jit(solution)/shard_map/ppermute | solution.py:406
  121.7 2.1 %collective-permute-start.17 = (f32[256,256]{1,0:T(8,128)S(1)}, f32[256,256]{1,0:T(8,128)S(1)}, u32[]{:S(2)}, u32[]{:S(2)}) collective-permute-start(f32[256,256]{1,0:T(8,128)S(1)} %add.28), channel_id=1, source_target_pairs={{0,4},{1,5},{2,6},{3,7},{4,0},{5,1},{6,2},{7,3},{8,12},{9,13},{10,... | collective-permute-start | bytes 786440 | tf_op jit(solution)/shard_map/ppermute | solution.py:408
  123.8 14.7 %collective-permute-done.13.near_ref = f32[512,256]{1,0:T(8,128)S(1)} collective-permute-done((f32[512,256]{1,0:T(8,128)S(1)}, f32[512,256]{1,0:T(8,128)S(1)}, u32[]{:S(2)}, u32[]{:S(2)}) %collective-permute-start.13) | collective-permute-done | bytes 524320 | tf_op jit(solution)/shard_map/ppermute | solution.py:406
  138.6 2.1 %collective-permute-start.14 = (f32[256,256]{1,0:T(8,128)S(1)}, f32[256,256]{1,0:T(8,128)S(1)}, u32[]{:S(2)}, u32[]{:S(2)}) collective-permute-start(f32[256,256]{1,0:T(8,128)S(1)} %add.27), channel_id=1, source_target_pairs={{0,4},{1,5},{2,6},{3,7},{4,0},{5,1},{6,2},{7,3},{8,12},{9,13},{10,... | collective-permute-start | bytes 786440 | tf_op jit(solution)/shard_map/ppermute | solution.py:408
  140.7 5.4 %collective-permute-done.19.near_ref = f32[512,256]{1,0:T(8,128)S(1)} collective-permute-done((f32[512,256]{1,0:T(8,128)S(1)}, f32[512,256]{1,0:T(8,128)S(1)}, u32[]{:S(2)}, u32[]{:S(2)}) %collective-permute-start.19) | collective-permute-done | bytes 524320 | tf_op jit(solution)/shard_map/ppermute | solution.py:406
  146.1 1.3 collective-permute-start.20
  147.4 15.0 %factor_first.1.in_ref = f32[256,512]{1,0:T(8,128)S(1)} custom-call(f32[768,128]{1,0:T(8,128)S(1)} %get-tuple-element.37.keep_ref, f32[768,128]{1,0:T(8,128)S(1)} %collective-permute-done.10.near_ref, f32[384,128]{1,0:T(8,128)S(1)} %collective-permute-done.11.far_ref), custom_call_target="tpu_custom_call" | custom-call | flops 10000000000 | bytes 1048576 | tf_op jit(solution)/shard_map/factor_first/pallas_call | solution.py:303
  162.4 14.8 %factor_last.1 = (f32[256,1024]{1,0:T(8,128)}, f32[256,256]{1,0:T(8,128)S(1)}) custom-call(f32[256,512]{1,0:T(8,128)S(1)} %factor_first.1.in_ref), custom_call_target="tpu_custom_call" | custom-call | flops 10000000000 | bytes 1048576 | tf_op jit(solution)/shard_map/factor_last/pallas_call | solution.py:318
  177.2 1.1 couple.3.whole_ref
  178.3 1.1 couple.4.whole_ref
  179.4 1.1 couple.5
  (35 shorter events, 0.6 us)
Async XLA Ops:
  4.5 12.7 %collective-permute-start.2 = (bf16[1024,256]{1,0:T(8,128)(2,1)}, bf16[1024,256]{1,0:T(8,128)(2,1)}, u32[]{:S(2)}, u32[]{:S(2)}) collective-permute-start(bf16[1024,256]{1,0:T(8,128)(2,1)} %mix.5), channel_id=1, source_target_pairs={{0,8},{8,0},{16,24},{24,16},{1,9},{9,1},{17,25},{25,17},{2,10},{10... | collective-permute-start | bytes 1572872 | tf_op jit(solution)/shard_map/ppermute | solution.py:383
  8.9 12.6 %collective-permute-start.6 = (bf16[1024,256]{1,0:T(8,128)(2,1)}, bf16[1024,256]{1,0:T(8,128)(2,1)S(1)}, u32[]{:S(2)}, u32[]{:S(2)}) collective-permute-start(bf16[1024,256]{1,0:T(8,128)(2,1)} %mix.7), channel_id=1, source_target_pairs={{0,8},{8,0},{16,24},{24,16},{1,9},{9,1},{17,25},{25,17},{2,10},{10... | collective-permute-start | bytes 1572872 | tf_op jit(solution)/shard_map/ppermute | solution.py:383
  12.8 4.5 %copy-start.5 = (bf16[1024,256]{1,0:T(8,128)(2,1)S(1)}, bf16[1024,256]{1,0:T(8,128)(2,1)}, u32[]{:S(2)}) copy-start(bf16[1024,256]{1,0:T(8,128)(2,1)} %mix.5) | copy-start | bytes 1572868
  12.8 8.7 %copy-start.3 = (bf16[1024,256]{1,0:T(8,128)(2,1)S(1)}, bf16[1024,256]{1,0:T(8,128)(2,1)}, u32[]{:S(2)}) copy-start(bf16[1024,256]{1,0:T(8,128)(2,1)} %mix.7) | copy-start | bytes 1572868
  12.8 12.3 %collective-permute-start = (bf16[1024,256]{1,0:T(8,128)(2,1)}, bf16[1024,256]{1,0:T(8,128)(2,1)}, u32[]{:S(2)}, u32[]{:S(2)}) collective-permute-start(bf16[1024,256]{1,0:T(8,128)(2,1)} %mix.4), channel_id=1, source_target_pairs={{0,8},{8,0},{16,24},{24,16},{1,9},{9,1},{17,25},{25,17},{2,10},{10... | collective-permute-start | bytes 1572872 | tf_op jit(solution)/shard_map/ppermute | solution.py:383
  17.1 4.7 %copy-start.4 = (bf16[1024,256]{1,0:T(8,128)(2,1)S(1)}, bf16[1024,256]{1,0:T(8,128)(2,1)}, u32[]{:S(2)}) copy-start(bf16[1024,256]{1,0:T(8,128)(2,1)} %mix.6) | copy-start | bytes 1572868
  17.2 4.7 %collective-permute-start.4 = (bf16[1024,256]{1,0:T(8,128)(2,1)}, bf16[1024,256]{1,0:T(8,128)(2,1)}, u32[]{:S(2)}, u32[]{:S(2)}) collective-permute-start(bf16[1024,256]{1,0:T(8,128)(2,1)} %mix.6), channel_id=1, source_target_pairs={{0,8},{8,0},{16,24},{24,16},{1,9},{9,1},{17,25},{25,17},{2,10},{10... | collective-permute-start | bytes 1572872 | tf_op jit(solution)/shard_map/ppermute | solution.py:383
  17.3 7.9 %copy-start.2 = (bf16[1024,256]{1,0:T(8,128)(2,1)S(1)}, bf16[1024,256]{1,0:T(8,128)(2,1)}, u32[]{:S(2)}) copy-start(bf16[1024,256]{1,0:T(8,128)(2,1)} %mix.4) | copy-start | bytes 1572868
  18.6 40.2 %collective-permute-start.3 = (bf16[1024,256]{1,0:T(8,128)(2,1)S(1)}, bf16[1024,256]{1,0:T(8,128)(2,1)}, u32[]{:S(2)}, u32[]{:S(2)}) collective-permute-start(bf16[1024,256]{1,0:T(8,128)(2,1)S(1)} %multiply_convert_fusion.2.own_ref), channel_id=1, source_target_pairs={{0,16},{8,24},{16,0},{24,8},{1,17},{9,25},{17,1},{25,9},{2,18},{10... | collective-permute-start | bytes 1572872 | tf_op jit(solution)/shard_map/ppermute | solution.py:395
  21.7 23.8 %collective-permute-start.7 = (bf16[1024,256]{1,0:T(8,128)(2,1)S(1)}, bf16[1024,256]{1,0:T(8,128)(2,1)S(1)}, u32[]{:S(2)}, u32[]{:S(2)}) collective-permute-start(bf16[1024,256]{1,0:T(8,128)(2,1)S(1)} %multiply_convert_fusion.own_ref), channel_id=1, source_target_pairs={{0,16},{8,24},{16,0},{24,8},{1,17},{9,25},{17,1},{25,9},{2,18},{10... | collective-permute-start | bytes 1572872 | tf_op jit(solution)/shard_map/ppermute | solution.py:395
  23.1 33.8 %collective-permute-start.5 = (bf16[1024,256]{1,0:T(8,128)(2,1)S(1)}, bf16[1024,256]{1,0:T(8,128)(2,1)}, u32[]{:S(2)}, u32[]{:S(2)}) collective-permute-start(bf16[1024,256]{1,0:T(8,128)(2,1)S(1)} %multiply_convert_fusion.1.own_ref), channel_id=1, source_target_pairs={{0,16},{8,24},{16,0},{24,8},{1,17},{9,25},{17,1},{25,9},{2,18},{10... | collective-permute-start | bytes 1572872 | tf_op jit(solution)/shard_map/ppermute | solution.py:395
  26.4 41.2 %collective-permute-start.1 = (bf16[1024,256]{1,0:T(8,128)(2,1)S(1)}, bf16[1024,256]{1,0:T(8,128)(2,1)}, u32[]{:S(2)}, u32[]{:S(2)}) collective-permute-start(bf16[1024,256]{1,0:T(8,128)(2,1)S(1)} %multiply_convert_fusion.3.own_ref), channel_id=1, source_target_pairs={{0,16},{8,24},{16,0},{24,8},{1,17},{9,25},{17,1},{25,9},{2,18},{10... | collective-permute-start | bytes 1572872 | tf_op jit(solution)/shard_map/ppermute | solution.py:395
  46.5 40.4 %collective-permute-start.9 = (bf16[1024,256]{1,0:T(8,128)(2,1)S(1)}, bf16[1024,256]{1,0:T(8,128)(2,1)S(1)}, u32[]{:S(2)}, u32[]{:S(2)}) collective-permute-start(bf16[1024,256]{1,0:T(8,128)(2,1)S(1)} %get-tuple-element.31.lead_ref.refs_2_), channel_id=1, source_target_pairs={{0,1},{1,0},{2,3},{3,2},{4,5},{5,4},{6,7},{7,6},{8,9},{9,8},{10,11... | collective-permute-start | bytes 1572872 | tf_op jit(solution)/shard_map/ppermute | solution.py:399
  60.6 10.6 %copy-start = (s32[2048]{0:T(1024)S(1)}, s32[2048]{0:T(1024)}, u32[]{:S(2)}) copy-start(s32[2048]{0:T(1024)} %param.7) | copy-start | bytes 24580
  60.6 10.6 %copy-start.1 = (s32[2048,1]{0,1:T(1,128)S(1)}, s32[2048,1]{0,1:T(1,128)}, u32[]{:S(2)}) copy-start(s32[2048,1]{0,1:T(1,128)} %param.8) | copy-start | bytes 24580
  60.6 32.8 %collective-permute-start.15 = (bf16[1024,256]{1,0:T(8,128)(2,1)S(1)}, bf16[1024,256]{1,0:T(8,128)(2,1)S(1)}, u32[]{:S(2)}, u32[]{:S(2)}) collective-permute-start(bf16[1024,256]{1,0:T(8,128)(2,1)S(1)} %get-tuple-element.43.refs_2_), channel_id=1, source_target_pairs={{0,1},{1,0},{2,3},{3,2},{4,5},{5,4},{6,7},{7,6},{8,9},{9,8},{10,11... | collective-permute-start | bytes 1572872 | tf_op jit(solution)/shard_map/ppermute | solution.py:399
  69.4 28.3 %collective-permute-start.12 = (bf16[1024,256]{1,0:T(8,128)(2,1)S(1)}, bf16[1024,256]{1,0:T(8,128)(2,1)S(1)}, u32[]{:S(2)}, u32[]{:S(2)}) collective-permute-start(bf16[1024,256]{1,0:T(8,128)(2,1)S(1)} %get-tuple-element.40.refs_2_), channel_id=1, source_target_pairs={{0,1},{1,0},{2,3},{3,2},{4,5},{5,4},{6,7},{7,6},{8,9},{9,8},{10,11... | collective-permute-start | bytes 1572872 | tf_op jit(solution)/shard_map/ppermute | solution.py:399
  72.9 13.9 %collective-permute-start.8 = (f32[4,1024]{1,0:T(4,128)S(1)}, f32[4,1024]{1,0:T(4,128)S(1)}, u32[]{:S(2)}, u32[]{:S(2)}) collective-permute-start(f32[4,1024]{1,0:T(4,128)S(1)} %get-tuple-element.34), channel_id=1, source_target_pairs={{0,1},{1,0},{2,3},{3,2},{4,5},{5,4},{6,7},{7,6},{8,9},{9,8},{10,11... | collective-permute-start | bytes 49160 | tf_op jit(solution)/shard_map/ppermute | solution.py:390
  73.3 29.8 %collective-permute-start.18 = (bf16[1024,256]{1,0:T(8,128)(2,1)S(1)}, bf16[1024,256]{1,0:T(8,128)(2,1)S(1)}, u32[]{:S(2)}, u32[]{:S(2)}) collective-permute-start(bf16[1024,256]{1,0:T(8,128)(2,1)S(1)} %get-tuple-element.46.refs_2_), channel_id=1, source_target_pairs={{0,1},{1,0},{2,3},{3,2},{4,5},{5,4},{6,7},{7,6},{8,9},{9,8},{10,11... | collective-permute-start | bytes 1572872 | tf_op jit(solution)/shard_map/ppermute | solution.py:399
  91.8 15.7 %collective-permute-start.10 = (f32[768,128]{1,0:T(8,128)S(1)}, f32[768,128]{1,0:T(8,128)S(1)}, u32[]{:S(2)}, u32[]{:S(2)}) collective-permute-start(f32[768,128]{1,0:T(8,128)S(1)} %get-tuple-element.38), channel_id=1, source_target_pairs={{0,2},{1,3},{2,0},{3,1},{4,6},{5,7},{6,4},{7,5},{8,10},{9,11},{10,... | collective-permute-start | bytes 1179656 | tf_op jit(solution)/shard_map/ppermute | solution.py:406
  97.1 24.5 %collective-permute-start.16 = (f32[512,256]{1,0:T(8,128)S(1)}, f32[512,256]{1,0:T(8,128)S(1)}, u32[]{:S(2)}, u32[]{:S(2)}) collective-permute-start(f32[512,256]{1,0:T(8,128)S(1)} %get-tuple-element.45), channel_id=1, source_target_pairs={{0,2},{1,3},{2,0},{3,1},{4,6},{5,7},{6,4},{7,5},{8,10},{9,11},{10,... | collective-permute-start | bytes 1572872 | tf_op jit(solution)/shard_map/ppermute | solution.py:406
  101.5 37.1 %collective-permute-start.13 = (f32[512,256]{1,0:T(8,128)S(1)}, f32[512,256]{1,0:T(8,128)S(1)}, u32[]{:S(2)}, u32[]{:S(2)}) collective-permute-start(f32[512,256]{1,0:T(8,128)S(1)} %get-tuple-element.42), channel_id=1, source_target_pairs={{0,2},{1,3},{2,0},{3,1},{4,6},{5,7},{6,4},{7,5},{8,10},{9,11},{10,... | collective-permute-start | bytes 1572872 | tf_op jit(solution)/shard_map/ppermute | solution.py:406
  107.0 39.1 %collective-permute-start.19 = (f32[512,256]{1,0:T(8,128)S(1)}, f32[512,256]{1,0:T(8,128)S(1)}, u32[]{:S(2)}, u32[]{:S(2)}) collective-permute-start(f32[512,256]{1,0:T(8,128)S(1)} %get-tuple-element.48), channel_id=1, source_target_pairs={{0,2},{1,3},{2,0},{3,1},{4,6},{5,7},{6,4},{7,5},{8,10},{9,11},{10,... | collective-permute-start | bytes 1572872 | tf_op jit(solution)/shard_map/ppermute | solution.py:406
  107.6 39.9 %collective-permute-start.11 = (f32[384,128]{1,0:T(8,128)S(1)}, f32[384,128]{1,0:T(8,128)S(1)}, u32[]{:S(2)}, u32[]{:S(2)}) collective-permute-start(f32[384,128]{1,0:T(8,128)S(1)} %add.26), channel_id=1, source_target_pairs={{0,4},{1,5},{2,6},{3,7},{4,0},{5,1},{6,2},{7,3},{8,12},{9,13},{10,... | collective-permute-start | bytes 589832 | tf_op jit(solution)/shard_map/ppermute | solution.py:408
  121.7 56.6 %collective-permute-start.17 = (f32[256,256]{1,0:T(8,128)S(1)}, f32[256,256]{1,0:T(8,128)S(1)}, u32[]{:S(2)}, u32[]{:S(2)}) collective-permute-start(f32[256,256]{1,0:T(8,128)S(1)} %add.28), channel_id=1, source_target_pairs={{0,4},{1,5},{2,6},{3,7},{4,0},{5,1},{6,2},{7,3},{8,12},{9,13},{10,... | collective-permute-start | bytes 786440 | tf_op jit(solution)/shard_map/ppermute | solution.py:408
  138.6 40.8 %collective-permute-start.14 = (f32[256,256]{1,0:T(8,128)S(1)}, f32[256,256]{1,0:T(8,128)S(1)}, u32[]{:S(2)}, u32[]{:S(2)}) collective-permute-start(f32[256,256]{1,0:T(8,128)S(1)} %add.27), channel_id=1, source_target_pairs={{0,4},{1,5},{2,6},{3,7},{4,0},{5,1},{6,2},{7,3},{8,12},{9,13},{10,... | collective-permute-start | bytes 786440 | tf_op jit(solution)/shard_map/ppermute | solution.py:408
  146.1 31.1 %collective-permute-start.20 = (f32[256,256]{1,0:T(8,128)S(1)}, f32[256,256]{1,0:T(8,128)S(1)}, u32[]{:S(2)}, u32[]{:S(2)}) collective-permute-start(f32[256,256]{1,0:T(8,128)S(1)} %add.29), channel_id=1, source_target_pairs={{0,4},{1,5},{2,6},{3,7},{4,0},{5,1},{6,2},{7,3},{8,12},{9,13},{10,... | collective-permute-start | bytes 786440 | tf_op jit(solution)/shard_map/ppermute | solution.py:408
where the time goes:
time: 181 us; the launch traced here: 180 us
  waiting for transfers between devices  74.8 us (41%)
  Pallas kernels  74.4 us (41%)
  starting transfers between devices  26.5 us (15%)
  other arithmetic  4.03 us (2%)
    ppermute x4, waiting for transfers between devices, per_device(): lax.ppermute(current[i], 'wide', [(w, w ^ wide // 2) for w in range(wide)])  32.4 us
    ppermute x4, waiting for transfers between devices, per_device(): near = lax.ppermute(send, 'blk', z_route(1))  31.6 us
    pallas_call x4, Pallas kernels, mix_chunk(): pl.pallas_call(mix_kernel, grid=(rows // size,), in_specs=[pl.BlockSpec((...  15.5 us
    pallas_call x4, Pallas kernels, partial_grams(): pl.pallas_call(functools.partial(gram_kernel, parts, packed), grid=(parts...  15.1 us
    pallas_call x1, Pallas kernels, factor_first(): pl.pallas_call(functools.partial(factor_first_kernel, scale), grid=(1,),...  15 us
    pallas_call x1, Pallas kernels, factor_last(): pl.pallas_call(factor_last_kernel, grid=(1,), in_specs=[pl.BlockSpec(stat...  14.8 us
    ppermute x1, waiting for transfers between devices, per_device(): owner_counts.append(lax.ppermute(counts[s], 'blk', x_shift(s)))  10.7 us
    ppermute x4, starting transfers between devices, per_device(): far = lax.ppermute(onward, 'blk', z_route(2))  8.17 us
  transfers between devices with their start and end apart: 21, of which 7 were waited for; matrix products, arithmetic and copies ran while one was open for 2% of the time, Pallas kernels for 38%

commit v1 on v0

--- a/solution.py
+++ b/solution.py
@@ -40,16 +40,20 @@
 
 
 def mix_kernel(signs_ref, had_ref, x_ref, out_ref):
-    signed = (had_ref[...].astype(F32) * signs_ref[...].astype(F32)).astype(BF16)
-    x = x_ref[...]
-    hi = x.astype(BF16)
-    rest = x - hi.astype(F32)
-    mid = rest.astype(BF16)
-    low = (rest - mid.astype(F32)).astype(BF16)
-    total = jnp.dot(signed, low, preferred_element_type=F32)
-    total = total + jnp.dot(signed, mid, preferred_element_type=F32)
-    total = total + jnp.dot(signed, hi, preferred_element_type=F32)
-    out_ref[...] = (total * (HB**-0.5)).astype(BF16)
+    rows = x_ref.shape[0]
+    size = had_ref.shape[0]
+    for b in range(rows // size):
+        part = pl.ds(b * size, size)
+        signed = (had_ref[...].astype(F32) * signs_ref[:, b * size : (b + 1) * size].astype(F32)).astype(BF16)
+        x = x_ref[part, :]
+        hi = x.astype(BF16)
+        rest = x - hi.astype(F32)
+        mid = rest.astype(BF16)
+        low = (rest - mid.astype(F32)).astype(BF16)
+        total = jnp.dot(signed, low, preferred_element_type=F32)
+        total = total + jnp.dot(signed, mid, preferred_element_type=F32)
+        total = total + jnp.dot(signed, hi, preferred_element_type=F32)
+        out_ref[part, :] = (total * (HB**-0.5)).astype(BF16)
 
 
 def mix_chunk(signs, had, flux, start, width):
@@ -58,13 +62,13 @@
     block = start // width
     return pl.pallas_call(
         mix_kernel,
-        grid=(rows // size,),
+        grid=(1,),
         in_specs=[
-            pl.BlockSpec((1, size), lambda i: (0, i)),
+            pl.BlockSpec((1, rows), lambda i: (0, 0)),
             pl.BlockSpec(had.shape, lambda i: (0, 0)),
-            pl.BlockSpec((size, width), lambda i: (i, block)),
+            pl.BlockSpec((rows, width), lambda i: (0, block)),
         ],
-        out_specs=pl.BlockSpec((size, width), lambda i: (i, 0)),
+        out_specs=pl.BlockSpec((rows, width), lambda i: (0, 0)),
         out_shape=jax.ShapeDtypeStruct((rows, width), BF16),
         cost_estimate=cost(2 * rows * width * size * 3, rows * width * 6),
         name="mix",
@@ -244,25 +248,33 @@
     )(keep, near)
 
 
-BAND = 32
-CUT = 4
+BAND = 64
+CUT = 2
+MICRO = 8
+
+
+def factor_band(tile):
+    row_id = lax.broadcasted_iota(jnp.int32, (BAND, 1), 0)
+    for first in range(0, BAND, MICRO):
+        spread = [jnp.broadcast_to(tile[:, first + t : first + t + 1], tile.shape) for t in range(MICRO)]
+        for t in range(MICRO):
+            j = first + t
+            r = lax.rsqrt(spread[t][j : j + 1, :])
+            row = tile[j : j + 1, :] * r
+            below = jnp.where(row_id > j, spread[t], 0.0)
+            for u in range(t + 1, MICRO):
+                spread[u] = spread[u] - below * (spread[u][j : j + 1, :] * (r * r))
+            tile = jnp.where(row_id == j, row, tile - below * (row * r))
+    return tile
 
 
 def eliminate(work, first, last):
     rb = lax.broadcasted_iota(jnp.int32, (BAND, BAND), 0)
     cb = lax.broadcasted_iota(jnp.int32, (BAND, BAND), 1)
     eye_b = (rb == cb).astype(F32)
-    row_id = lax.broadcasted_iota(jnp.int32, (BAND, 1), 0)
     for k in range(first, last):
         lo, hi = k * BAND, (k + 1) * BAND
-        tile = jnp.concatenate([work[lo:hi, lo:hi], eye_b], axis=1)
-        for j in range(BAND):
-            pivot = tile[j : j + 1, j : j + 1]
-            r = lax.rsqrt(pivot)
-            r = r * (1.5 - 0.5 * pivot * r * r)
-            row = tile[j : j + 1, :] * r
-            column = tile[:, j : j + 1] * r
-            tile = jnp.where(row_id == j, row, jnp.where(row_id > j, tile - column * row, tile))
+        tile = factor_band(jnp.concatenate([work[lo:hi, lo:hi], eye_b], axis=1))
         inv = jnp.where(rb >= cb, tile[:, BAND:], 0.0)
         full = jnp.dot(inv, work[lo:hi, lo:], precision=HIGHEST, preferred_element_type=F32)
         if hi < PANEL:
@@ -378,16 +390,16 @@
     for i in chunks:
         start, width = CHUNKS[i]
         current.append(mix_chunk(signs, had, flux_rows, start, width))
+    counts = count_samples(sample_rows, sample_owner, nx, rows, me_z, me_x)
+    owner_counts = [counts[0]]
+    for s in range(1, nx):
+        owner_counts.append(lax.ppermute(counts[s], "blk", x_shift(s)))
+
     for level in range(levels - 1):
         for i in chunks:
             partner = lax.ppermute(current[i], "wide", [(w, w ^ (1 << level)) for w in range(wide)])
             own = current[i].astype(F32)
             current[i] = ((partner.astype(F32) + own * level_sign(level)) * SQRT_HALF).astype(BF16)
-
-    counts = count_samples(sample_rows, sample_owner, nx, rows, me_z, me_x)
-    owner_counts = [counts[0]]
-    for s in range(1, nx):
-        owner_counts.append(lax.ppermute(counts[s], "blk", x_shift(s)))
 
     whole, sources = None, []
     for i in chunks:

time: 181 us -> 164 us (0.906)
  Pallas kernels: 74.4 us -> 50.2 us
  waiting for transfers between devices: 74.8 us -> 81.9 us
    pallas_call x1, Pallas kernels: 15 us -> 4.99 us  [factor_first(): pl.pallas_call(functools.partial(factor_first_kernel, scale), grid=(1,),...]
    pallas_call x1, Pallas kernels: 14.8 us -> 5.09 us  [factor_last(): pl.pallas_call(factor_last_kernel, grid=(1,), in_specs=[pl.BlockSpec(stat...]
    ppermute x4, waiting for transfers between devices: 0.01 us -> 7.32 us  [per_device(): far = lax.ppermute(onward, 'blk', z_route(2))]
    pallas_call x4, Pallas kernels: 15.5 us -> 11 us  [mix_chunk(): pl.pallas_call(mix_kernel, grid=(1,), in_specs=[pl.BlockSpec((1, rows), l...]
  transfers between devices with their start and end apart: 21 -> 21, of which waited for: 7 -> 8; matrix products, arithmetic and copies ran while one was open for 2% -> 2% of each run, Pallas kernels for 38% -> 28%
where the time goes in v1:
time: 164 us
  waiting for transfers between devices  81.9 us (50%)
  Pallas kernels  50.2 us (31%)
  starting transfers between devices  26.7 us (16%)
  other arithmetic  4.03 us (2%)
    ppermute x4, waiting for transfers between devices, per_device(): lax.ppermute(current[i], 'wide', [(w, w ^ wide // 2) for w in range(wide)])  32.4 us
    ppermute x4, waiting for transfers between devices, per_device(): near = lax.ppermute(send, 'blk', z_route(1))  31.4 us
    pallas_call x4, Pallas kernels, partial_grams(): pl.pallas_call(functools.partial(gram_kernel, parts, packed), grid=(parts...  15.2 us
    pallas_call x4, Pallas kernels, mix_chunk(): pl.pallas_call(mix_kernel, grid=(1,), in_specs=[pl.BlockSpec((1, rows), l...  11 us
    ppermute x1, waiting for transfers between devices, per_device(): owner_counts.append(lax.ppermute(counts[s], 'blk', x_shift(s)))  10.7 us
    ppermute x4, starting transfers between devices, per_device(): far = lax.ppermute(onward, 'blk', z_route(2))  8.29 us
    ppermute x4, starting transfers between devices, per_device(): sources[i].append(lax.ppermute(current[i], 'blk', x_shift(s)))  7.4 us
    ppermute x4, waiting for transfers between devices, per_device(): far = lax.ppermute(onward, 'blk', z_route(2))  7.32 us
  transfers between devices with their start and end apart: 21, of which 8 were waited for; matrix products, arithmetic and copies ran while one was open for 2% of the time, Pallas kernels for 28%

profile of v1, /device:TPU:0, one launch (start us, length us, event | category | flops | bytes accessed | tf_op | source)
XLA Modules:
  0.0 163.6 jit_solution(4538502995706026574)
XLA Ops:
  0.6 2.7 %mix.5 = bf16[1024,256]{1,0:T(8,128)(2,1)} custom-call(s32[1,1024]{1,0:T(1,128)} %bitcast.8, bf16[256,256]{1,0:T(8,128)(2,1)} %constant.20.clone.had_ref, f32[1024,1024]{1,0:T(8,128)} %x_ref.7), custom_call_target="tpu_custom_call" | custom-call | flops 402653184 | bytes 1572864 | tf_op jit(solution)/shard_map/mix/pallas_call | solution.py:63
  3.4 0.5 collective-permute-start.2
  3.9 2.7 %mix.7 = bf16[1024,256]{1,0:T(8,128)(2,1)} custom-call(s32[1,1024]{1,0:T(1,128)} %bitcast.9, bf16[256,256]{1,0:T(8,128)(2,1)} %constant.20.clone.had_ref, f32[1024,1024]{1,0:T(8,128)} %x_ref.7), custom_call_target="tpu_custom_call" | custom-call | flops 402653184 | bytes 1572864 | tf_op jit(solution)/shard_map/mix/pallas_call | solution.py:63
  6.6 2.7 %mix.4 = bf16[1024,256]{1,0:T(8,128)(2,1)} custom-call(s32[1,1024]{1,0:T(1,128)} %bitcast.10, bf16[256,256]{1,0:T(8,128)(2,1)} %constant.20.clone.had_ref, f32[1024,1024]{1,0:T(8,128)} %x_ref.7), custom_call_target="tpu_custom_call" | custom-call | flops 402653184 | bytes 1572864 | tf_op jit(solution)/shard_map/mix/pallas_call | solution.py:63
  9.4 0.5 collective-permute-start
  9.9 2.7 %mix.6 = bf16[1024,256]{1,0:T(8,128)(2,1)} custom-call(s32[1,1024]{1,0:T(1,128)} %bitcast.11, bf16[256,256]{1,0:T(8,128)(2,1)} %constant.20.clone.had_ref, f32[1024,1024]{1,0:T(8,128)} %x_ref.7), custom_call_target="tpu_custom_call" | custom-call | flops 402653184 | bytes 1572864 | tf_op jit(solution)/shard_map/mix/pallas_call | solution.py:63
  12.7 1.3 multiply_convert_fusion.2.own_ref
  14.0 3.0 %collective-permute-start.3 = (bf16[1024,256]{1,0:T(8,128)(2,1)S(1)}, bf16[1024,256]{1,0:T(8,128)(2,1)}, u32[]{:S(2)}, u32[]{:S(2)}) collective-permute-start(bf16[1024,256]{1,0:T(8,128)(2,1)S(1)} %multiply_convert_fusion.2.own_ref), channel_id=1, source_target_pairs={{0,16},{8,24},{16,0},{24,8},{1,17},{9,25},{17,1},{25,9},{2,18},{10... | collective-permute-start | bytes 1572872 | tf_op jit(solution)/shard_map/ppermute | solution.py:407
  17.3 1.2 multiply_convert_fusion.1.own_ref
  18.5 2.1 %collective-permute-start.5 = (bf16[1024,256]{1,0:T(8,128)(2,1)S(1)}, bf16[1024,256]{1,0:T(8,128)(2,1)}, u32[]{:S(2)}, u32[]{:S(2)}) collective-permute-start(bf16[1024,256]{1,0:T(8,128)(2,1)S(1)} %multiply_convert_fusion.1.own_ref), channel_id=1, source_target_pairs={{0,16},{8,24},{16,0},{24,8},{1,17},{9,25},{17,1},{25,9},{2,18},{10... | collective-permute-start | bytes 1572872 | tf_op jit(solution)/shard_map/ppermute | solution.py:407
  20.6 1.2 multiply_convert_fusion.3.own_ref
  21.9 19.1 %collective-permute-done.7.other_ref = bf16[1024,256]{1,0:T(8,128)(2,1)S(1)} collective-permute-done((bf16[1024,256]{1,0:T(8,128)(2,1)S(1)}, bf16[1024,256]{1,0:T(8,128)(2,1)S(1)}, u32[]{:S(2)}, u32[]{:S(2)}) %collective-permute-start.7) | collective-permute-done | bytes 524320 | tf_op jit(solution)/shard_map/ppermute | solution.py:407
  41.0 0.9 join.4
  41.9 2.0 %collective-permute-start.9 = (bf16[1024,256]{1,0:T(8,128)(2,1)S(1)}, bf16[1024,256]{1,0:T(8,128)(2,1)S(1)}, u32[]{:S(2)}, u32[]{:S(2)}) collective-permute-start(bf16[1024,256]{1,0:T(8,128)(2,1)S(1)} %get-tuple-element.31.lead_ref.refs_2_), channel_id=1, source_target_pairs={{0,1},{1,0},{2,3},{3,2},{4,5},{5,4},{6,7},{7,6},{8,9},{9,8},{10,11... | collective-permute-start | bytes 1572872 | tf_op jit(solution)/shard_map/ppermute | solution.py:411
  43.9 8.4 %collective-permute-done.5.other_ref = bf16[1024,256]{1,0:T(8,128)(2,1)} collective-permute-done((bf16[1024,256]{1,0:T(8,128)(2,1)S(1)}, bf16[1024,256]{1,0:T(8,128)(2,1)}, u32[]{:S(2)}, u32[]{:S(2)}) %collective-permute-start.5) | collective-permute-done | bytes 524320 | tf_op jit(solution)/shard_map/ppermute | solution.py:407
  52.3 1.9 %join.5 = (bf16[1024,256]{1,0:T(8,128)(2,1)S(1)}, bf16[1024,1024]{1,0:T(8,128)(2,1)}) custom-call(f32[1]{0:T(128)} %bitcast.sign_ref, bf16[1024,256]{1,0:T(8,128)(2,1)S(1)} %multiply_convert_fusion.1.own_ref, bf16[1024,256]{1,0:T(8,128)(2,1)} %collective-permute-done.5.other_ref, ...), custom_call_target="tpu_custom_call", output_to_operand_aliasing={{1}: (3, {})} | custom-call | flops 1048576 | bytes 2097152 | tf_op jit(solution)/shard_map/join/pallas_call | solution.py:95
  54.2 1.9 %join.6 = (bf16[1024,256]{1,0:T(8,128)(2,1)S(1)}, bf16[1024,1024]{1,0:T(8,128)(2,1)}) custom-call(f32[1]{0:T(128)} %bitcast.sign_ref, bf16[1024,256]{1,0:T(8,128)(2,1)S(1)} %multiply_convert_fusion.2.own_ref, bf16[1024,256]{1,0:T(8,128)(2,1)} %collective-permute-done.3.other_ref, ...), custom_call_target="tpu_custom_call", output_to_operand_aliasing={{1}: (3, {})} | custom-call | flops 1048576 | bytes 2097152 | tf_op jit(solution)/shard_map/join/pallas_call | solution.py:95
  56.1 2.0 %collective-permute-start.15 = (bf16[1024,256]{1,0:T(8,128)(2,1)S(1)}, bf16[1024,256]{1,0:T(8,128)(2,1)S(1)}, u32[]{:S(2)}, u32[]{:S(2)}) collective-permute-start(bf16[1024,256]{1,0:T(8,128)(2,1)S(1)} %get-tuple-element.43.refs_2_), channel_id=1, source_target_pairs={{0,1},{1,0},{2,3},{3,2},{4,5},{5,4},{6,7},{7,6},{8,9},{9,8},{10,11... | collective-permute-start | bytes 1572872 | tf_op jit(solution)/shard_map/ppermute | solution.py:411
  58.1 4.9 %collective-permute-done.1.other_ref = bf16[1024,256]{1,0:T(8,128)(2,1)} collective-permute-done((bf16[1024,256]{1,0:T(8,128)(2,1)S(1)}, bf16[1024,256]{1,0:T(8,128)(2,1)}, u32[]{:S(2)}, u32[]{:S(2)}) %collective-permute-start.1) | collective-permute-done | bytes 524320 | tf_op jit(solution)/shard_map/ppermute | solution.py:407
  63.0 1.9 %join.7 = (bf16[1024,256]{1,0:T(8,128)(2,1)S(1)}, bf16[1024,1024]{1,0:T(8,128)(2,1)}) custom-call(f32[1]{0:T(128)} %bitcast.sign_ref, bf16[1024,256]{1,0:T(8,128)(2,1)S(1)} %multiply_convert_fusion.3.own_ref, bf16[1024,256]{1,0:T(8,128)(2,1)} %collective-permute-done.1.other_ref, ...), custom_call_target="tpu_custom_call", output_to_operand_aliasing={{1}: (3, {})} | custom-call | flops 1048576 | bytes 2097152 | tf_op jit(solution)/shard_map/join/pallas_call | solution.py:95
  64.8 1.7 %collective-permute-start.12 = (bf16[1024,256]{1,0:T(8,128)(2,1)S(1)}, bf16[1024,256]{1,0:T(8,128)(2,1)S(1)}, u32[]{:S(2)}, u32[]{:S(2)}) collective-permute-start(bf16[1024,256]{1,0:T(8,128)(2,1)S(1)} %get-tuple-element.40.refs_2_), channel_id=1, source_target_pairs={{0,1},{1,0},{2,3},{3,2},{4,5},{5,4},{6,7},{7,6},{8,9},{9,8},{10,11... | collective-permute-start | bytes 1572872 | tf_op jit(solution)/shard_map/ppermute | solution.py:411
  66.6 1.7 %counts.1 = (f32[4,1024]{1,0:T(4,128)S(1)}, f32[4,1024]{1,0:T(4,128)S(1)}) custom-call(s32[2]{0:T(128)S(1)} %pad_add_fusion.me_ref, s32[1,2048]{1,0:T(1,128)S(1)} %bitcast.6, s32[1,2048]{1,0:T(1,128)S(1)} %bitcast.7), custom_call_target="tpu_custom_call" | custom-call | flops 33554432 | bytes 32768 | tf_op jit(solution)/shard_map/counts/pallas_call | solution.py:131
  68.4 0.3 collective-permute-start.8
  68.7 1.7 %collective-permute-start.18 = (bf16[1024,256]{1,0:T(8,128)(2,1)S(1)}, bf16[1024,256]{1,0:T(8,128)(2,1)S(1)}, u32[]{:S(2)}, u32[]{:S(2)}) collective-permute-start(bf16[1024,256]{1,0:T(8,128)(2,1)S(1)} %get-tuple-element.46.refs_2_), channel_id=1, source_target_pairs={{0,1},{1,0},{2,3},{3,2},{4,5},{5,4},{6,7},{7,6},{8,9},{9,8},{10,11... | collective-permute-start | bytes 1572872 | tf_op jit(solution)/shard_map/ppermute | solution.py:411
  70.4 1.2 weigh.2
  71.6 10.7 %collective-permute-done.8.counts_ref = f32[4,1024]{1,0:T(4,128)S(1)} collective-permute-done((f32[4,1024]{1,0:T(4,128)S(1)}, f32[4,1024]{1,0:T(4,128)S(1)}, u32[]{:S(2)}, u32[]{:S(2)}) %collective-permute-start.8) | collective-permute-done | bytes 16416 | tf_op jit(solution)/shard_map/ppermute | solution.py:396
  82.3 1.2 weigh.3
  83.5 3.7 %grams.4 = (f32[768,128]{1,0:T(8,128)S(1)}, f32[768,128]{1,0:T(8,128)S(1)}) custom-call(bf16[1024,1024]{1,0:T(8,128)(2,1)S(1)} %get-tuple-element.32.refs_0_, bf16[1024,1024]{1,0:T(8,128)(2,1)S(1)} %get-tuple-element.33.refs_1_, bf16[1024,256]{1,0:T(8,128)(2,1)S(1)} %get-tuple-element.31.lead_ref.refs_2_, bf16[1024,1024]{1,0:T(8,128)(2,1)S(1)} %get-tuple-element.35.refs_3_, ...), custom_call_target="tpu_custom_call" | custom-call | flops 2147483648 | bytes 9437184 | tf_op jit(solution)/shard_map/grams/pallas_call | solution.py:219
  87.2 1.6 collective-permute-start.10
  88.8 3.7 %grams.6 = (f32[512,256]{1,0:T(8,128)S(1)}, f32[512,256]{1,0:T(8,128)S(1)}) custom-call(bf16[1024,1024]{1,0:T(8,128)(2,1)S(1)} %get-tuple-element.32.refs_0_, bf16[1024,1024]{1,0:T(8,128)(2,1)S(1)} %get-tuple-element.33.refs_1_, bf16[1024,256]{1,0:T(8,128)(2,1)S(1)} %get-tuple-element.43.refs_2_, bf16[1024,1024]{1,0:T(8,128)(2,1)S(1)} %get-tuple-element.35.refs_3_, ...), custom_call_target="tpu_custom_call" | custom-call | flops 2147483648 | bytes 9437184 | tf_op jit(solution)/shard_map/grams/pallas_call | solution.py:219
  92.6 0.6 collective-permute-start.16
  93.1 3.7 %grams.5 = (f32[512,256]{1,0:T(8,128)S(1)}, f32[512,256]{1,0:T(8,128)S(1)}) custom-call(bf16[1024,1024]{1,0:T(8,128)(2,1)S(1)} %get-tuple-element.32.refs_0_, bf16[1024,1024]{1,0:T(8,128)(2,1)S(1)} %get-tuple-element.33.refs_1_, bf16[1024,256]{1,0:T(8,128)(2,1)S(1)} %get-tuple-element.40.refs_2_, bf16[1024,1024]{1,0:T(8,128)(2,1)S(1)} %get-tuple-element.35.refs_3_, ...), custom_call_target="tpu_custom_call" | custom-call | flops 2147483648 | bytes 9437184 | tf_op jit(solution)/shard_map/grams/pallas_call | solution.py:219
  96.9 1.6 collective-permute-start.13
  98.5 4.0 %grams.7 = (f32[512,256]{1,0:T(8,128)S(1)}, f32[512,256]{1,0:T(8,128)S(1)}) custom-call(bf16[1024,1024]{1,0:T(8,128)(2,1)S(1)} %get-tuple-element.32.refs_0_, bf16[1024,1024]{1,0:T(8,128)(2,1)S(1)} %get-tuple-element.33.refs_1_, bf16[1024,256]{1,0:T(8,128)(2,1)S(1)} %get-tuple-element.46.refs_2_, bf16[1024,1024]{1,0:T(8,128)(2,1)S(1)} %get-tuple-element.35.refs_3_, ...), custom_call_target="tpu_custom_call" | custom-call | flops 2147483648 | bytes 9437184 | tf_op jit(solution)/shard_map/grams/pallas_call | solution.py:219
  102.4 0.6 collective-permute-start.19
  103.0 2.6 %collective-permute-start.11 = (f32[384,128]{1,0:T(8,128)S(1)}, f32[384,128]{1,0:T(8,128)S(1)}, u32[]{:S(2)}, u32[]{:S(2)}) collective-permute-start(f32[384,128]{1,0:T(8,128)S(1)} %add.26), channel_id=1, source_target_pairs={{0,4},{1,5},{2,6},{3,7},{4,0},{5,1},{6,2},{7,3},{8,12},{9,13},{10,... | collective-permute-start | bytes 589832 | tf_op jit(solution)/shard_map/ppermute | solution.py:420
  105.6 11.4 %collective-permute-done.16.near_ref = f32[512,256]{1,0:T(8,128)S(1)} collective-permute-done((f32[512,256]{1,0:T(8,128)S(1)}, f32[512,256]{1,0:T(8,128)S(1)}, u32[]{:S(2)}, u32[]{:S(2)}) %collective-permute-start.16) | collective-permute-done | bytes 524320 | tf_op jit(solution)/shard_map/ppermute | solution.py:418
  117.1 2.2 %collective-permute-start.17 = (f32[256,256]{1,0:T(8,128)S(1)}, f32[256,256]{1,0:T(8,128)S(1)}, u32[]{:S(2)}, u32[]{:S(2)}) collective-permute-start(f32[256,256]{1,0:T(8,128)S(1)} %add.28), channel_id=1, source_target_pairs={{0,4},{1,5},{2,6},{3,7},{4,0},{5,1},{6,2},{7,3},{8,12},{9,13},{10,... | collective-permute-start | bytes 786440 | tf_op jit(solution)/shard_map/ppermute | solution.py:420
  119.3 14.6 %collective-permute-done.13.near_ref = f32[512,256]{1,0:T(8,128)S(1)} collective-permute-done((f32[512,256]{1,0:T(8,128)S(1)}, f32[512,256]{1,0:T(8,128)S(1)}, u32[]{:S(2)}, u32[]{:S(2)}) %collective-permute-start.13) | collective-permute-done | bytes 524320 | tf_op jit(solution)/shard_map/ppermute | solution.py:418
  133.9 2.2 %collective-permute-start.14 = (f32[256,256]{1,0:T(8,128)S(1)}, f32[256,256]{1,0:T(8,128)S(1)}, u32[]{:S(2)}, u32[]{:S(2)}) collective-permute-start(f32[256,256]{1,0:T(8,128)S(1)} %add.27), channel_id=1, source_target_pairs={{0,4},{1,5},{2,6},{3,7},{4,0},{5,1},{6,2},{7,3},{8,12},{9,13},{10,... | collective-permute-start | bytes 786440 | tf_op jit(solution)/shard_map/ppermute | solution.py:420
  136.1 5.4 %collective-permute-done.19.near_ref = f32[512,256]{1,0:T(8,128)S(1)} collective-permute-done((f32[512,256]{1,0:T(8,128)S(1)}, f32[512,256]{1,0:T(8,128)S(1)}, u32[]{:S(2)}, u32[]{:S(2)}) %collective-permute-start.19) | collective-permute-done | bytes 524320 | tf_op jit(solution)/shard_map/ppermute | solution.py:418
  141.5 1.3 collective-permute-start.20
  142.8 5.0 %factor_first.1.in_ref = f32[256,512]{1,0:T(8,128)S(1)} custom-call(f32[768,128]{1,0:T(8,128)S(1)} %get-tuple-element.37.keep_ref, f32[768,128]{1,0:T(8,128)S(1)} %collective-permute-done.10.near_ref, f32[384,128]{1,0:T(8,128)S(1)} %collective-permute-done.11.far_ref), custom_call_target="tpu_custom_call" | custom-call | flops 10000000000 | bytes 1048576 | tf_op jit(solution)/shard_map/factor_first/pallas_call | solution.py:315
  147.8 5.1 %factor_last.1 = (f32[256,1024]{1,0:T(8,128)}, f32[256,256]{1,0:T(8,128)S(1)}) custom-call(f32[256,512]{1,0:T(8,128)S(1)} %factor_first.1.in_ref), custom_call_target="tpu_custom_call" | custom-call | flops 10000000000 | bytes 1048576 | tf_op jit(solution)/shard_map/factor_last/pallas_call | solution.py:330
  152.9 7.3 %collective-permute-done.20.far_ref = f32[256,256]{1,0:T(8,128)S(1)} collective-permute-done((f32[256,256]{1,0:T(8,128)S(1)}, f32[256,256]{1,0:T(8,128)S(1)}, u32[]{:S(2)}, u32[]{:S(2)}) %collective-permute-start.20) | collective-permute-done | bytes 262176 | tf_op jit(solution)/shard_map/ppermute | solution.py:420
  160.2 1.1 couple.3.whole_ref
  161.3 1.1 couple.4.whole_ref
  162.5 1.1 couple.5
  (35 shorter events, 0.8 us)
Async XLA Ops:
  3.4 9.3 %collective-permute-start.2 = (bf16[1024,256]{1,0:T(8,128)(2,1)}, bf16[1024,256]{1,0:T(8,128)(2,1)}, u32[]{:S(2)}, u32[]{:S(2)}) collective-permute-start(bf16[1024,256]{1,0:T(8,128)(2,1)} %mix.5), channel_id=1, source_target_pairs={{0,8},{8,0},{16,24},{24,16},{1,9},{9,1},{17,25},{25,17},{2,10},{10... | collective-permute-start | bytes 1572872 | tf_op jit(solution)/shard_map/ppermute | solution.py:400
  6.6 10.4 %collective-permute-start.6 = (bf16[1024,256]{1,0:T(8,128)(2,1)}, bf16[1024,256]{1,0:T(8,128)(2,1)S(1)}, u32[]{:S(2)}, u32[]{:S(2)}) collective-permute-start(bf16[1024,256]{1,0:T(8,128)(2,1)} %mix.7), channel_id=1, source_target_pairs={{0,8},{8,0},{16,24},{24,16},{1,9},{9,1},{17,25},{25,17},{2,10},{10... | collective-permute-start | bytes 1572872 | tf_op jit(solution)/shard_map/ppermute | solution.py:400
  9.4 3.3 %copy-start.5 = (bf16[1024,256]{1,0:T(8,128)(2,1)S(1)}, bf16[1024,256]{1,0:T(8,128)(2,1)}, u32[]{:S(2)}) copy-start(bf16[1024,256]{1,0:T(8,128)(2,1)} %mix.5) | copy-start | bytes 1572868
  9.4 7.6 %copy-start.3 = (bf16[1024,256]{1,0:T(8,128)(2,1)S(1)}, bf16[1024,256]{1,0:T(8,128)(2,1)}, u32[]{:S(2)}) copy-start(bf16[1024,256]{1,0:T(8,128)(2,1)} %mix.7) | copy-start | bytes 1572868
  9.4 11.2 %collective-permute-start = (bf16[1024,256]{1,0:T(8,128)(2,1)}, bf16[1024,256]{1,0:T(8,128)(2,1)}, u32[]{:S(2)}, u32[]{:S(2)}) collective-permute-start(bf16[1024,256]{1,0:T(8,128)(2,1)} %mix.4), channel_id=1, source_target_pairs={{0,8},{8,0},{16,24},{24,16},{1,9},{9,1},{17,25},{25,17},{2,10},{10... | collective-permute-start | bytes 1572872 | tf_op jit(solution)/shard_map/ppermute | solution.py:400
  12.6 4.7 %copy-start.4 = (bf16[1024,256]{1,0:T(8,128)(2,1)S(1)}, bf16[1024,256]{1,0:T(8,128)(2,1)}, u32[]{:S(2)}) copy-start(bf16[1024,256]{1,0:T(8,128)(2,1)} %mix.6) | copy-start | bytes 1572868
  12.6 4.7 %collective-permute-start.4 = (bf16[1024,256]{1,0:T(8,128)(2,1)}, bf16[1024,256]{1,0:T(8,128)(2,1)}, u32[]{:S(2)}, u32[]{:S(2)}) collective-permute-start(bf16[1024,256]{1,0:T(8,128)(2,1)} %mix.6), channel_id=1, source_target_pairs={{0,8},{8,0},{16,24},{24,16},{1,9},{9,1},{17,25},{25,17},{2,10},{10... | collective-permute-start | bytes 1572872 | tf_op jit(solution)/shard_map/ppermute | solution.py:400
  12.7 7.9 %copy-start.2 = (bf16[1024,256]{1,0:T(8,128)(2,1)S(1)}, bf16[1024,256]{1,0:T(8,128)(2,1)}, u32[]{:S(2)}) copy-start(bf16[1024,256]{1,0:T(8,128)(2,1)} %mix.4) | copy-start | bytes 1572868
  14.0 40.2 %collective-permute-start.3 = (bf16[1024,256]{1,0:T(8,128)(2,1)S(1)}, bf16[1024,256]{1,0:T(8,128)(2,1)}, u32[]{:S(2)}, u32[]{:S(2)}) collective-permute-start(bf16[1024,256]{1,0:T(8,128)(2,1)S(1)} %multiply_convert_fusion.2.own_ref), channel_id=1, source_target_pairs={{0,16},{8,24},{16,0},{24,8},{1,17},{9,25},{17,1},{25,9},{2,18},{10... | collective-permute-start | bytes 1572872 | tf_op jit(solution)/shard_map/ppermute | solution.py:407
  17.2 23.8 %collective-permute-start.7 = (bf16[1024,256]{1,0:T(8,128)(2,1)S(1)}, bf16[1024,256]{1,0:T(8,128)(2,1)S(1)}, u32[]{:S(2)}, u32[]{:S(2)}) collective-permute-start(bf16[1024,256]{1,0:T(8,128)(2,1)S(1)} %multiply_convert_fusion.own_ref), channel_id=1, source_target_pairs={{0,16},{8,24},{16,0},{24,8},{1,17},{9,25},{17,1},{25,9},{2,18},{10... | collective-permute-start | bytes 1572872 | tf_op jit(solution)/shard_map/ppermute | solution.py:407
  18.5 33.8 %collective-permute-start.5 = (bf16[1024,256]{1,0:T(8,128)(2,1)S(1)}, bf16[1024,256]{1,0:T(8,128)(2,1)}, u32[]{:S(2)}, u32[]{:S(2)}) collective-permute-start(bf16[1024,256]{1,0:T(8,128)(2,1)S(1)} %multiply_convert_fusion.1.own_ref), channel_id=1, source_target_pairs={{0,16},{8,24},{16,0},{24,8},{1,17},{9,25},{17,1},{25,9},{2,18},{10... | collective-permute-start | bytes 1572872 | tf_op jit(solution)/shard_map/ppermute | solution.py:407
  21.8 41.2 %collective-permute-start.1 = (bf16[1024,256]{1,0:T(8,128)(2,1)S(1)}, bf16[1024,256]{1,0:T(8,128)(2,1)}, u32[]{:S(2)}, u32[]{:S(2)}) collective-permute-start(bf16[1024,256]{1,0:T(8,128)(2,1)S(1)} %multiply_convert_fusion.3.own_ref), channel_id=1, source_target_pairs={{0,16},{8,24},{16,0},{24,8},{1,17},{9,25},{17,1},{25,9},{2,18},{10... | collective-permute-start | bytes 1572872 | tf_op jit(solution)/shard_map/ppermute | solution.py:407
  41.9 40.4 %collective-permute-start.9 = (bf16[1024,256]{1,0:T(8,128)(2,1)S(1)}, bf16[1024,256]{1,0:T(8,128)(2,1)S(1)}, u32[]{:S(2)}, u32[]{:S(2)}) collective-permute-start(bf16[1024,256]{1,0:T(8,128)(2,1)S(1)} %get-tuple-element.31.lead_ref.refs_2_), channel_id=1, source_target_pairs={{0,1},{1,0},{2,3},{3,2},{4,5},{5,4},{6,7},{7,6},{8,9},{9,8},{10,11... | collective-permute-start | bytes 1572872 | tf_op jit(solution)/shard_map/ppermute | solution.py:411
  56.1 10.6 %copy-start = (s32[2048]{0:T(1024)S(1)}, s32[2048]{0:T(1024)}, u32[]{:S(2)}) copy-start(s32[2048]{0:T(1024)} %param.7) | copy-start | bytes 24580
  56.1 10.6 %copy-start.1 = (s32[2048,1]{0,1:T(1,128)S(1)}, s32[2048,1]{0,1:T(1,128)}, u32[]{:S(2)}) copy-start(s32[2048,1]{0,1:T(1,128)} %param.8) | copy-start | bytes 24580
  56.1 32.7 %collective-permute-start.15 = (bf16[1024,256]{1,0:T(8,128)(2,1)S(1)}, bf16[1024,256]{1,0:T(8,128)(2,1)S(1)}, u32[]{:S(2)}, u32[]{:S(2)}) collective-permute-start(bf16[1024,256]{1,0:T(8,128)(2,1)S(1)} %get-tuple-element.43.refs_2_), channel_id=1, source_target_pairs={{0,1},{1,0},{2,3},{3,2},{4,5},{5,4},{6,7},{7,6},{8,9},{9,8},{10,11... | collective-permute-start | bytes 1572872 | tf_op jit(solution)/shard_map/ppermute | solution.py:411
  64.8 28.3 %collective-permute-start.12 = (bf16[1024,256]{1,0:T(8,128)(2,1)S(1)}, bf16[1024,256]{1,0:T(8,128)(2,1)S(1)}, u32[]{:S(2)}, u32[]{:S(2)}) collective-permute-start(bf16[1024,256]{1,0:T(8,128)(2,1)S(1)} %get-tuple-element.40.refs_2_), channel_id=1, source_target_pairs={{0,1},{1,0},{2,3},{3,2},{4,5},{5,4},{6,7},{7,6},{8,9},{9,8},{10,11... | collective-permute-start | bytes 1572872 | tf_op jit(solution)/shard_map/ppermute | solution.py:411
  68.4 13.9 %collective-permute-start.8 = (f32[4,1024]{1,0:T(4,128)S(1)}, f32[4,1024]{1,0:T(4,128)S(1)}, u32[]{:S(2)}, u32[]{:S(2)}) collective-permute-start(f32[4,1024]{1,0:T(4,128)S(1)} %get-tuple-element.34), channel_id=1, source_target_pairs={{0,1},{1,0},{2,3},{3,2},{4,5},{5,4},{6,7},{7,6},{8,9},{9,8},{10,11... | collective-permute-start | bytes 49160 | tf_op jit(solution)/shard_map/ppermute | solution.py:396
  68.7 29.8 %collective-permute-start.18 = (bf16[1024,256]{1,0:T(8,128)(2,1)S(1)}, bf16[1024,256]{1,0:T(8,128)(2,1)S(1)}, u32[]{:S(2)}, u32[]{:S(2)}) collective-permute-start(bf16[1024,256]{1,0:T(8,128)(2,1)S(1)} %get-tuple-element.46.refs_2_), channel_id=1, source_target_pairs={{0,1},{1,0},{2,3},{3,2},{4,5},{5,4},{6,7},{7,6},{8,9},{9,8},{10,11... | collective-permute-start | bytes 1572872 | tf_op jit(solution)/shard_map/ppermute | solution.py:411
  87.2 15.8 %collective-permute-start.10 = (f32[768,128]{1,0:T(8,128)S(1)}, f32[768,128]{1,0:T(8,128)S(1)}, u32[]{:S(2)}, u32[]{:S(2)}) collective-permute-start(f32[768,128]{1,0:T(8,128)S(1)} %get-tuple-element.38), channel_id=1, source_target_pairs={{0,2},{1,3},{2,0},{3,1},{4,6},{5,7},{6,4},{7,5},{8,10},{9,11},{10,... | collective-permute-start | bytes 1179656 | tf_op jit(solution)/shard_map/ppermute | solution.py:418
  92.6 24.5 %collective-permute-start.16 = (f32[512,256]{1,0:T(8,128)S(1)}, f32[512,256]{1,0:T(8,128)S(1)}, u32[]{:S(2)}, u32[]{:S(2)}) collective-permute-start(f32[512,256]{1,0:T(8,128)S(1)} %get-tuple-element.45), channel_id=1, source_target_pairs={{0,2},{1,3},{2,0},{3,1},{4,6},{5,7},{6,4},{7,5},{8,10},{9,11},{10,... | collective-permute-start | bytes 1572872 | tf_op jit(solution)/shard_map/ppermute | solution.py:418
  96.9 37.0 %collective-permute-start.13 = (f32[512,256]{1,0:T(8,128)S(1)}, f32[512,256]{1,0:T(8,128)S(1)}, u32[]{:S(2)}, u32[]{:S(2)}) collective-permute-start(f32[512,256]{1,0:T(8,128)S(1)} %get-tuple-element.42), channel_id=1, source_target_pairs={{0,2},{1,3},{2,0},{3,1},{4,6},{5,7},{6,4},{7,5},{8,10},{9,11},{10,... | collective-permute-start | bytes 1572872 | tf_op jit(solution)/shard_map/ppermute | solution.py:418
  102.4 39.1 %collective-permute-start.19 = (f32[512,256]{1,0:T(8,128)S(1)}, f32[512,256]{1,0:T(8,128)S(1)}, u32[]{:S(2)}, u32[]{:S(2)}) collective-permute-start(f32[512,256]{1,0:T(8,128)S(1)} %get-tuple-element.48), channel_id=1, source_target_pairs={{0,2},{1,3},{2,0},{3,1},{4,6},{5,7},{6,4},{7,5},{8,10},{9,11},{10,... | collective-permute-start | bytes 1572872 | tf_op jit(solution)/shard_map/ppermute | solution.py:418
  103.0 39.8 %collective-permute-start.11 = (f32[384,128]{1,0:T(8,128)S(1)}, f32[384,128]{1,0:T(8,128)S(1)}, u32[]{:S(2)}, u32[]{:S(2)}) collective-permute-start(f32[384,128]{1,0:T(8,128)S(1)} %add.26), channel_id=1, source_target_pairs={{0,4},{1,5},{2,6},{3,7},{4,0},{5,1},{6,2},{7,3},{8,12},{9,13},{10,... | collective-permute-start | bytes 589832 | tf_op jit(solution)/shard_map/ppermute | solution.py:420
  117.1 44.3 %collective-permute-start.17 = (f32[256,256]{1,0:T(8,128)S(1)}, f32[256,256]{1,0:T(8,128)S(1)}, u32[]{:S(2)}, u32[]{:S(2)}) collective-permute-start(f32[256,256]{1,0:T(8,128)S(1)} %add.28), channel_id=1, source_target_pairs={{0,4},{1,5},{2,6},{3,7},{4,0},{5,1},{6,2},{7,3},{8,12},{9,13},{10,... | collective-permute-start | bytes 786440 | tf_op jit(solution)/shard_map/ppermute | solution.py:420
  133.9 28.5 %collective-permute-start.14 = (f32[256,256]{1,0:T(8,128)S(1)}, f32[256,256]{1,0:T(8,128)S(1)}, u32[]{:S(2)}, u32[]{:S(2)}) collective-permute-start(f32[256,256]{1,0:T(8,128)S(1)} %add.27), channel_id=1, source_target_pairs={{0,4},{1,5},{2,6},{3,7},{4,0},{5,1},{6,2},{7,3},{8,12},{9,13},{10,... | collective-permute-start | bytes 786440 | tf_op jit(solution)/shard_map/ppermute | solution.py:420
  141.5 18.7 %collective-permute-start.20 = (f32[256,256]{1,0:T(8,128)S(1)}, f32[256,256]{1,0:T(8,128)S(1)}, u32[]{:S(2)}, u32[]{:S(2)}) collective-permute-start(f32[256,256]{1,0:T(8,128)S(1)} %add.29), channel_id=1, source_target_pairs={{0,4},{1,5},{2,6},{3,7},{4,0},{5,1},{6,2},{7,3},{8,12},{9,13},{10,... | collective-permute-start | bytes 786440 | tf_op jit(solution)/shard_map/ppermute | solution.py:420

commit v2 on v1

--- a/solution.py
+++ b/solution.py
@@ -11,7 +11,8 @@
 PANEL = 256
 HB = 128
 NZ = 4
-CHUNKS = ((0, 256), (256, 256), (512, 256), (768, 256))
+LEAD = ((0, 128), (128, 128))
+CHUNKS = ((256, 256), (512, 256), (768, 128), (896, 128))
 SQRT_HALF = 0.7071067811865476
 HIGHEST = lax.Precision.HIGHEST
 F32 = jnp.float32
@@ -56,23 +57,45 @@
         out_ref[part, :] = (total * (HB**-0.5)).astype(BF16)
 
 
-def mix_chunk(signs, had, flux, start, width):
+def mix_columns(signs, had, flux, first, blocks):
     rows = flux.shape[0]
-    size = had.shape[0]
-    block = start // width
     return pl.pallas_call(
         mix_kernel,
-        grid=(1,),
+        grid=(blocks,),
         in_specs=[
             pl.BlockSpec((1, rows), lambda i: (0, 0)),
             pl.BlockSpec(had.shape, lambda i: (0, 0)),
-            pl.BlockSpec((rows, width), lambda i: (0, block)),
+            pl.BlockSpec((rows, PANEL), lambda i: (0, i + first)),
         ],
-        out_specs=pl.BlockSpec((rows, width), lambda i: (0, 0)),
-        out_shape=jax.ShapeDtypeStruct((rows, width), BF16),
-        cost_estimate=cost(2 * rows * width * size * 3, rows * width * 6),
+        out_specs=pl.BlockSpec((None, rows, PANEL), lambda i: (i, 0, 0)),
+        out_shape=jax.ShapeDtypeStruct((blocks, rows, PANEL), BF16),
+        cost_estimate=cost(2 * blocks * rows * PANEL * had.shape[0] * 3, blocks * rows * PANEL * 6),
         name="mix",
     )(signs, had, flux)
+
+
+def join_split_kernel(places, sign_ref, own_ref, other_ref, *out_refs):
+    total = (other_ref[...].astype(F32) + own_ref[...].astype(F32) * sign_ref[0]) * SQRT_HALF
+    total = total.astype(BF16)
+    for (block, offset, width), ref in zip(places, out_refs):
+        ref[...] = total[block, :, offset : offset + width]
+
+
+def join_split(own, other, sign, chunks):
+    blocks, rows, wide = own.shape
+    tile = rows // 4
+    base = chunks[0][0]
+    places = tuple(((start - base) // wide, (start - base) % wide, width) for start, width in chunks)
+    spec = pl.BlockSpec((blocks, tile, wide), lambda i: (0, i, 0))
+    return pl.pallas_call(
+        functools.partial(join_split_kernel, places),
+        grid=(rows // tile,),
+        in_specs=[pl.BlockSpec(memory_space=pltpu.SMEM), spec, spec],
+        out_specs=tuple(pl.BlockSpec((tile, width), lambda i: (i, 0)) for _, width in chunks),
+        out_shape=tuple(jax.ShapeDtypeStruct((rows, width), BF16) for _, width in chunks),
+        cost_estimate=cost(4 * blocks * rows * wide, 6 * blocks * rows * wide),
+        name="join",
+    )(sign.reshape(1), own, other)
 
 
 def join_kernel(sign_ref, own_ref, other_ref, *refs):
@@ -138,8 +161,8 @@
     )(jnp.stack([me_z, me_x]), sample_rows.reshape(1, listed), sample_owner.reshape(1, listed))
 
 
-def weigh_kernel(counts_ref, lead_ref, hi_ref, lo_ref):
-    lead = lead_ref[...].astype(F32).T
+def weigh_kernel(counts_ref, left_ref, right_ref, hi_ref, lo_ref):
+    lead = jnp.concatenate([left_ref[...].astype(F32).T, right_ref[...].astype(F32).T], axis=0)
     for q in range(NZ):
         part = pl.ds(q * PANEL, PANEL)
         weighed = lead * counts_ref[q : q + 1, :]
@@ -148,21 +171,21 @@
         lo_ref[part, :] = (weighed - hi.astype(F32)).astype(BF16)
 
 
-def weigh(counts, lead):
-    rows = lead.shape[0]
+def weigh(counts, left, right):
+    rows = left.shape[0]
     tile = rows // 2
     out = pl.BlockSpec((NZ * PANEL, tile), lambda i: (0, i))
     shape = jax.ShapeDtypeStruct((NZ * PANEL, rows), BF16)
     return pl.pallas_call(
         weigh_kernel,
         grid=(rows // tile,),
-        in_specs=[pl.BlockSpec((NZ, tile), lambda i: (0, i)), pl.BlockSpec((tile, PANEL), lambda i: (i, 0))],
+        in_specs=[pl.BlockSpec((NZ, tile), lambda i: (0, i))] + [pl.BlockSpec((tile, PANEL // 2), lambda i: (i, 0))] * 2,
         out_specs=(out, out),
         out_shape=(shape, shape),
         compiler_params=params(),
         cost_estimate=cost(rows * PANEL * 16, rows * PANEL * 18),
         name="weigh",
-    )(counts, lead)
+    )(counts, left, right)
 
 
 GRAM_TILES = 2
@@ -176,12 +199,13 @@
     def _():
         acc[...] = jnp.zeros_like(acc)
 
+    each = (len(refs) - 3) // parts
     for p in range(parts):
-        hi_ref, lo_ref, rows_ref = refs[3 * p : 3 * p + 3]
+        hi_ref, lo_ref, *rows_refs = refs[each * p : each * (p + 1)]
 
         @pl.when(step // GRAM_TILES == p)
-        def _(hi_ref=hi_ref, lo_ref=lo_ref, rows_ref=rows_ref):
-            rows = rows_ref[...]
+        def _(hi_ref=hi_ref, lo_ref=lo_ref, rows_refs=rows_refs):
+            rows = jnp.concatenate([ref[...] for ref in rows_refs], axis=1)
             low = jnp.dot(lo_ref[...], rows, preferred_element_type=F32)
             acc[...] += low + jnp.dot(hi_ref[...], rows, preferred_element_type=F32)
 
@@ -201,19 +225,21 @@
 
 def partial_grams(weights, chunk_rows, packed):
     parts = len(chunk_rows)
-    rows, width = chunk_rows[0].shape
+    rows = chunk_rows[0][0].shape[0]
+    width = sum(piece.shape[1] for piece in chunk_rows[0])
     tile = rows // GRAM_TILES
     half = NZ // 2
     shape = (half * (PANEL + PANEL // 2), PANEL // 2) if packed else (half * PANEL, width)
     operands, specs = [], []
-    for p, ((hi, lo), block) in enumerate(zip(weights, chunk_rows)):
-        operands += [hi, lo, block]
+    for p, ((hi, lo), pieces) in enumerate(zip(weights, chunk_rows)):
+        operands += [hi, lo, *pieces]
 
         def place(k, p=p):
             return jnp.clip(k - p * GRAM_TILES, 0, GRAM_TILES - 1)
 
         weight_spec = pl.BlockSpec((NZ * PANEL, tile), lambda k, place=place: (0, place(k)))
-        specs += [weight_spec, weight_spec, pl.BlockSpec((tile, width), lambda k, place=place: (place(k), 0))]
+        specs += [weight_spec, weight_spec]
+        specs += [pl.BlockSpec((tile, piece.shape[1]), lambda k, place=place: (place(k), 0)) for piece in pieces]
     out = pl.BlockSpec(shape, lambda k: (0, 0))
     out_shape = jax.ShapeDtypeStruct(shape, F32)
     return pl.pallas_call(
@@ -385,35 +411,44 @@
     def level_sign(level):
         return jnp.where((me_w >> level) & 1 == 1, -1.0, 1.0).astype(F32)
 
-    chunks = range(len(CHUNKS))
-    current = []
-    for i in chunks:
-        start, width = CHUNKS[i]
-        current.append(mix_chunk(signs, had, flux_rows, start, width))
+    def last_level(own, start, whole):
+        partner = lax.ppermute(own, "wide", [(w, w ^ (wide // 2)) for w in range(wide)])
+        own, whole = join_last(own, partner, level_sign(levels - 1), start, columns, whole)
+        pieces = [own]
+        for s in range(1, nx):
+            pieces.append(lax.ppermute(own, "blk", x_shift(s)))
+        return pieces, whole
+
+    def first_levels(current, chunks):
+        for level in range(levels - 1):
+            partner = lax.ppermute(current, "wide", [(w, w ^ (1 << level)) for w in range(wide)])
+            if level == levels - 2:
+                return join_split(current, partner, level_sign(level), chunks)
+            own = current.astype(F32)
+            current = ((partner.astype(F32) + own * level_sign(level)) * SQRT_HALF).astype(BF16)
+
+    mixed = mix_columns(signs, had, flux_rows, 0, 1)
+    lead = first_levels(mixed, LEAD)
     counts = count_samples(sample_rows, sample_owner, nx, rows, me_z, me_x)
     owner_counts = [counts[0]]
     for s in range(1, nx):
         owner_counts.append(lax.ppermute(counts[s], "blk", x_shift(s)))
-
-    for level in range(levels - 1):
-        for i in chunks:
-            partner = lax.ppermute(current[i], "wide", [(w, w ^ (1 << level)) for w in range(wide)])
-            own = current[i].astype(F32)
-            current[i] = ((partner.astype(F32) + own * level_sign(level)) * SQRT_HALF).astype(BF16)
-
-    whole, sources = None, []
-    for i in chunks:
-        start, width = CHUNKS[i]
-        partner = lax.ppermute(current[i], "wide", [(w, w ^ (wide // 2)) for w in range(wide)])
-        current[i], whole = join_last(current[i], partner, level_sign(levels - 1), start, columns, whole)
-        sources.append([current[i]])
-        for s in range(1, nx):
-            sources[i].append(lax.ppermute(current[i], "blk", x_shift(s)))
+    mixed = mix_columns(signs, had, flux_rows, 1, columns // PANEL - 1)
+    rest = first_levels(mixed, CHUNKS)
+
+    lead_pieces, whole = [], None
+    for i, (start, _) in enumerate(LEAD):
+        pieces, whole = last_level(lead[i], start, whole)
+        lead_pieces.append(pieces)
+    sources = [[[pieces[p] for pieces in lead_pieces] for p in range(nx)]]
+    for i, (start, _) in enumerate(CHUNKS):
+        pieces, whole = last_level(rest[i], start, whole)
+        sources.append([[piece] for piece in pieces])
 
     weights, grams = [], []
     for p in range(nx):
-        weights.append(weigh(owner_counts[p], sources[0][p]))
-    for i in chunks:
+        weights.append(weigh(owner_counts[p], *sources[0][p]))
+    for i in range(len(CHUNKS) + 1):
         keep, send = partial_grams(weights, sources[i], i == 0)
         near = lax.ppermute(send, "blk", z_route(1))
         onward = far_sum(keep, near)
@@ -421,8 +456,8 @@
         grams.append((keep, near, far))
     state = factor_first(*grams[0], scale)
     sketch, inverse = factor_last(state, columns)
-    for i in chunks[1:]:
-        sketch = couple(inverse, *grams[i], sketch, CHUNKS[i][0], scale)
+    for i, (start, _) in enumerate(CHUNKS):
+        sketch = couple(inverse, *grams[i + 1], sketch, start, scale)
     return whole, sketch
 
 

time: 164 us -> 153 us (0.933)
  waiting for transfers between devices: 81.9 us -> 60.6 us
  Pallas kernels: 50.2 us -> 56.6 us
  starting transfers between devices: 26.7 us -> 31.7 us
  other arithmetic: 4.03 us -> 0.07 us
  local copies, waits for them, and re-layouts: 0.02 us -> 2.72 us
    ppermute x4 -> x5, waiting for transfers between devices: 31.4 us -> 16.3 us  [per_device(): near = lax.ppermute(send, 'blk', z_route(1))]
    ppermute x1, waiting for transfers between devices: 10.7 us -> 1.33 us  [per_device(): owner_counts.append(lax.ppermute(counts[s], 'blk', x_shift(s)))]
    ppermute x4 -> x5, waiting for transfers between devices: 7.32 us -> 11.8 us  [per_device(): far = lax.ppermute(onward, 'blk', z_route(2))]
    convert_element_type x4 -> x0, other arithmetic: 3.96 us -> none  [per_device(): ((partner.astype(F32) + own * level_sign(level)) * SQRT_HALF).astype(BF16)]
    pallas_call x4, Pallas kernels: 11 us -> 14.7 us  [the longest x2 7.5 us: mix_columns(): pl.pallas_call(mix_kernel, grid=(blocks,), in_specs=[pl.BlockSpec((1, row...]
    pallas_call x4 -> x5, Pallas kernels: 15.2 us -> 18.6 us  [partial_grams(): pl.pallas_call(functools.partial(gram_kernel, parts, packed), grid=(parts...]
    unnamed x12 -> x18, local copies, waits for them, and re-layouts: 0.02 us -> 2.72 us
    ppermute x4 -> x5, starting transfers between devices: 4.31 us -> 6.93 us  [per_device(): near = lax.ppermute(send, 'blk', z_route(1))]
  transfers between devices with their start and end apart: 21 -> 25, of which waited for: 8 -> 11; matrix products, arithmetic and copies ran while one was open for 2% -> 0% of each run, Pallas kernels for 28% -> 33%
where the time goes in v2:
time: 153 us
  waiting for transfers between devices  60.6 us (40%)
  Pallas kernels  56.6 us (37%)
  starting transfers between devices  31.7 us (21%)
  local copies, waits for them, and re-layouts  2.72 us (2%)
    ppermute x6, waiting for transfers between devices, last_level(): lax.ppermute(own, 'wide', [(w, w ^ wide // 2) for w in range(wide)])  26.4 us
    pallas_call x5, Pallas kernels, partial_grams(): pl.pallas_call(functools.partial(gram_kernel, parts, packed), grid=(parts...  18.6 us
    ppermute x5, waiting for transfers between devices, per_device(): near = lax.ppermute(send, 'blk', z_route(1))  16.3 us
    ppermute x5, waiting for transfers between devices, per_device(): far = lax.ppermute(onward, 'blk', z_route(2))  11.8 us
    ppermute x5, starting transfers between devices, per_device(): far = lax.ppermute(onward, 'blk', z_route(2))  8.44 us
    pallas_call x2, Pallas kernels, mix_columns(): pl.pallas_call(mix_kernel, grid=(blocks,), in_specs=[pl.BlockSpec((1, row...  7.5 us
    ppermute x6, starting transfers between devices, last_level(): pieces.append(lax.ppermute(own, 'blk', x_shift(s)))  7.22 us
    pallas_call x2, Pallas kernels, join_split(): pl.pallas_call(functools.partial(join_split_kernel, places), grid=(rows /...  7.19 us
  transfers between devices with their start and end apart: 25, of which 11 were waited for; matrix products, arithmetic and copies ran while one was open for 0% of the time, Pallas kernels for 33%

profile of v2, /device:TPU:0, one launch (start us, length us, event | category | flops | bytes accessed | tf_op | source)
XLA Modules:
  0.0 152.5 jit_solution(14798617249354830713)
XLA Ops:
  0.6 4.8 %mix.2.own_ref = bf16[3,1024,256]{2,1,0:T(8,128)(2,1)} custom-call(s32[1,1024]{1,0:T(1,128)} %bitcast.9, bf16[256,256]{1,0:T(8,128)(2,1)} %constant.18.clone.had_ref, f32[1024,1024]{1,0:T(8,128)} %x_ref.3), custom_call_target="tpu_custom_call" | custom-call | flops 1207959552 | bytes 4718592 | tf_op jit(solution)/shard_map/mix/pallas_call | solution.py:62
  5.9 2.7 %mix.3.own_ref = bf16[1,1024,256]{2,1,0:T(8,128)(2,1)} custom-call(s32[1,1024]{1,0:T(1,128)} %bitcast.10, bf16[256,256]{1,0:T(8,128)(2,1)} %constant.18.clone.had_ref, f32[1024,1024]{1,0:T(8,128)} %x_ref.3), custom_call_target="tpu_custom_call" | custom-call | flops 402653184 | bytes 1572864 | tf_op jit(solution)/shard_map/mix/pallas_call | solution.py:62
  8.6 2.1 %collective-permute-done.5.other_ref = bf16[1,1024,256]{2,1,0:T(8,128)(2,1)S(1)} collective-permute-done((bf16[1,1024,256]{2,1,0:T(8,128)(2,1)}, bf16[1,1024,256]{2,1,0:T(8,128)(2,1)S(1)}, u32[]{:S(2)}, u32[]{:S(2)}) %collective-permute-start.5) | collective-permute-done | bytes 524320 | tf_op jit(solution)/shard_map/ppermute | solution.py:424
  11.5 3.3 %join.9 = (bf16[1024,128]{1,0:T(8,128)(2,1)}, bf16[1024,128]{1,0:T(8,128)(2,1)}) custom-call(f32[1]{0:T(128)} %bitcast.1.sign_ref, bf16[1,1024,256]{2,1,0:T(8,128)(2,1)} %mix.3.own_ref, bf16[1,1024,256]{2,1,0:T(8,128)(2,1)} %copy-done.8), custom_call_target="tpu_custom_call" | custom-call | flops 1048576 | bytes 1572864 | tf_op jit(solution)/shard_map/join/pallas_call | solution.py:90
  14.9 2.6 %collective-permute-start.7 = (bf16[1024,128]{1,0:T(8,128)(2,1)}, bf16[1024,128]{1,0:T(8,128)(2,1)S(1)}, u32[]{:S(2)}, u32[]{:S(2)}) collective-permute-start(bf16[1024,128]{1,0:T(8,128)(2,1)} %get-tuple-element.43.own_ref), channel_id=1, source_target_pairs={{0,16},{8,24},{16,0},{24,8},{1,17},{9,25},{17,1},{25,9},{2,18},{10... | collective-permute-start | bytes 786440 | tf_op jit(solution)/shard_map/ppermute | solution.py:415
  17.6 7.3 %collective-permute-done.7.other_ref = bf16[1024,128]{1,0:T(8,128)(2,1)S(1)} collective-permute-done((bf16[1024,128]{1,0:T(8,128)(2,1)}, bf16[1024,128]{1,0:T(8,128)(2,1)S(1)}, u32[]{:S(2)}, u32[]{:S(2)}) %collective-permute-start.7) | collective-permute-done | bytes 262176 | tf_op jit(solution)/shard_map/ppermute | solution.py:415
  24.9 0.9 copy-done.2
  26.6 3.6 %collective-permute-done.6.other_ref = bf16[1024,128]{1,0:T(8,128)(2,1)S(1)} collective-permute-done((bf16[1024,128]{1,0:T(8,128)(2,1)}, bf16[1024,128]{1,0:T(8,128)(2,1)S(1)}, u32[]{:S(2)}, u32[]{:S(2)}) %collective-permute-start.6) | collective-permute-done | bytes 262176 | tf_op jit(solution)/shard_map/ppermute | solution.py:415
  30.2 0.9 copy-done.5
  31.9 1.7 %collective-permute-start.10 = (bf16[1024,128]{1,0:T(8,128)(2,1)S(1)}, bf16[1024,128]{1,0:T(8,128)(2,1)S(1)}, u32[]{:S(2)}, u32[]{:S(2)}) collective-permute-start(bf16[1024,128]{1,0:T(8,128)(2,1)S(1)} %get-tuple-element.52.right_ref.refs_3_), channel_id=1, source_target_pairs={{0,1},{1,0},{2,3},{3,2},{4,5},{5,4},{6,7},{7,6},{8,9},{9,8},{10,11... | collective-permute-start | bytes 786440 | tf_op jit(solution)/shard_map/ppermute | solution.py:419
  33.9 3.9 %join.8 = (bf16[1024,256]{1,0:T(8,128)(2,1)}, bf16[1024,256]{1,0:T(8,128)(2,1)}, bf16[1024,128]{1,0:T(8,128)(2,1)}, bf16[1024,128]{1,0:T(8,128)(2,1)}) custom-call(f32[1]{0:T(128)} %bitcast.1.sign_ref, bf16[3,1024,256]{2,1,0:T(8,128)(2,1)} %mix.2.own_ref, bf16[3,1024,256]{2,1,0:T(8,128)(2,1)} %collective-permute-done.other_ref), custom_call_target="tpu_custom_call" | custom-call | flops 3145728 | bytes 4718592 | tf_op jit(solution)/shard_map/join/pallas_call | solution.py:90
  37.8 1.8 %collective-permute-start.4 = (bf16[1024,256]{1,0:T(8,128)(2,1)}, bf16[1024,256]{1,0:T(8,128)(2,1)S(1)}, u32[]{:S(2)}, u32[]{:S(2)}) collective-permute-start(bf16[1024,256]{1,0:T(8,128)(2,1)} %get-tuple-element.41.own_ref), channel_id=1, source_target_pairs={{0,16},{8,24},{16,0},{24,8},{1,17},{9,25},{17,1},{25,9},{2,18},{10... | collective-permute-start | bytes 1572872 | tf_op jit(solution)/shard_map/ppermute | solution.py:415
  39.9 1.7 %counts.1 = (f32[4,1024]{1,0:T(4,128)S(1)}, f32[4,1024]{1,0:T(4,128)S(1)}) custom-call(s32[2]{0:T(128)S(1)} %pad_add_fusion.me_ref, s32[1,2048]{1,0:T(1,128)S(1)} %bitcast.7, s32[1,2048]{1,0:T(1,128)S(1)} %bitcast.8), custom_call_target="tpu_custom_call" | custom-call | flops 33554432 | bytes 32768 | tf_op jit(solution)/shard_map/counts/pallas_call | solution.py:154
  41.7 1.7 %collective-permute-start.8 = (f32[4,1024]{1,0:T(4,128)S(1)}, f32[4,1024]{1,0:T(4,128)S(1)}, u32[]{:S(2)}, u32[]{:S(2)}) collective-permute-start(f32[4,1024]{1,0:T(4,128)S(1)} %get-tuple-element.55), channel_id=1, source_target_pairs={{0,1},{1,0},{2,3},{3,2},{4,5},{5,4},{6,7},{7,6},{8,9},{9,8},{10,11... | collective-permute-start | bytes 49160 | tf_op jit(solution)/shard_map/ppermute | solution.py:435
  43.4 1.1 weigh.2
  44.6 1.3 collective-permute-done.8.counts_ref
  45.9 1.1 weigh.3
  47.0 1.5 %collective-permute-start.1 = (bf16[1024,128]{1,0:T(8,128)(2,1)}, bf16[1024,128]{1,0:T(8,128)(2,1)S(1)}, u32[]{:S(2)}, u32[]{:S(2)}) collective-permute-start(bf16[1024,128]{1,0:T(8,128)(2,1)} %get-tuple-element.38.own_ref), channel_id=1, source_target_pairs={{0,16},{8,24},{16,0},{24,8},{1,17},{9,25},{17,1},{25,9},{2,18},{10... | collective-permute-start | bytes 786440 | tf_op jit(solution)/shard_map/ppermute | solution.py:415
  49.1 3.7 %grams.5 = (f32[768,128]{1,0:T(8,128)S(1)}, f32[768,128]{1,0:T(8,128)S(1)}) custom-call(bf16[1024,1024]{1,0:T(8,128)(2,1)S(1)} %get-tuple-element.53.refs_0_, bf16[1024,1024]{1,0:T(8,128)(2,1)S(1)} %get-tuple-element.54.refs_1_, bf16[1024,128]{1,0:T(8,128)(2,1)S(1)} %get-tuple-element.51.left_ref.refs_2_, ...), custom_call_target="tpu_custom_call" | custom-call | flops 2147483648 | bytes 9437184 | tf_op jit(solution)/shard_map/grams/pallas_call | solution.py:245
  52.9 1.6 %collective-permute-start.11 = (f32[768,128]{1,0:T(8,128)S(1)}, f32[768,128]{1,0:T(8,128)S(1)}, u32[]{:S(2)}, u32[]{:S(2)}) collective-permute-start(f32[768,128]{1,0:T(8,128)S(1)} %get-tuple-element.59), channel_id=1, source_target_pairs={{0,2},{1,3},{2,0},{3,1},{4,6},{5,7},{6,4},{7,5},{8,10},{9,11},{10,... | collective-permute-start | bytes 1179656 | tf_op jit(solution)/shard_map/ppermute | solution.py:453
  54.5 0.9 join.12
  55.4 8.7 %collective-permute-done.3.other_ref = bf16[1024,256]{1,0:T(8,128)(2,1)S(1)} collective-permute-done((bf16[1024,256]{1,0:T(8,128)(2,1)}, bf16[1024,256]{1,0:T(8,128)(2,1)S(1)}, u32[]{:S(2)}, u32[]{:S(2)}) %collective-permute-start.3) | collective-permute-done | bytes 524320 | tf_op jit(solution)/shard_map/ppermute | solution.py:415
  64.1 0.9 join.13
  65.0 1.7 %collective-permute-start.19 = (bf16[1024,256]{1,0:T(8,128)(2,1)S(1)}, bf16[1024,256]{1,0:T(8,128)(2,1)S(1)}, u32[]{:S(2)}, u32[]{:S(2)}) collective-permute-start(bf16[1024,256]{1,0:T(8,128)(2,1)S(1)} %get-tuple-element.67.refs_2_), channel_id=1, source_target_pairs={{0,1},{1,0},{2,3},{3,2},{4,5},{5,4},{6,7},{7,6},{8,9},{9,8},{10,11... | collective-permute-start | bytes 1572872 | tf_op jit(solution)/shard_map/ppermute | solution.py:419
  66.7 6.9 %collective-permute-done.2.other_ref = bf16[1024,128]{1,0:T(8,128)(2,1)S(1)} collective-permute-done((bf16[1024,128]{1,0:T(8,128)(2,1)}, bf16[1024,128]{1,0:T(8,128)(2,1)S(1)}, u32[]{:S(2)}, u32[]{:S(2)}) %collective-permute-start.2) | collective-permute-done | bytes 262176 | tf_op jit(solution)/shard_map/ppermute | solution.py:415
  74.4 1.4 collective-permute-start.16
  77.2 1.4 collective-permute-start.22
  78.6 2.6 %collective-permute-start.12 = (f32[384,128]{1,0:T(8,128)S(1)}, f32[384,128]{1,0:T(8,128)S(1)}, u32[]{:S(2)}, u32[]{:S(2)}) collective-permute-start(f32[384,128]{1,0:T(8,128)S(1)} %add.7), channel_id=1, source_target_pairs={{0,4},{1,5},{2,6},{3,7},{4,0},{5,1},{6,2},{7,3},{8,12},{9,13},{10,... | collective-permute-start | bytes 589832 | tf_op jit(solution)/shard_map/ppermute | solution.py:455
  81.3 2.2 %collective-permute-done.16.refs_5_ = bf16[1024,128]{1,0:T(8,128)(2,1)S(1)} collective-permute-done((bf16[1024,128]{1,0:T(8,128)(2,1)S(1)}, bf16[1024,128]{1,0:T(8,128)(2,1)S(1)}, u32[]{:S(2)}, u32[]{:S(2)}) %collective-permute-start.16) | collective-permute-done | bytes 262176 | tf_op jit(solution)/shard_map/ppermute | solution.py:419
  83.5 3.7 %grams.7 = (f32[512,128]{1,0:T(8,128)S(1)}, f32[512,128]{1,0:T(8,128)S(1)}) custom-call(bf16[1024,1024]{1,0:T(8,128)(2,1)S(1)} %get-tuple-element.53.refs_0_, bf16[1024,1024]{1,0:T(8,128)(2,1)S(1)} %get-tuple-element.54.refs_1_, bf16[1024,128]{1,0:T(8,128)(2,1)S(1)} %get-tuple-element.64.refs_2_, bf16[1024,1024]{1,0:T(8,128)(2,1)S(1)} %get-tuple-element.56.refs_4_.refs_3_, ...), custom_call_target="tpu_custom_call" | custom-call | flops 1073741824 | bytes 8912896 | tf_op jit(solution)/shard_map/grams/pallas_call | solution.py:245
  87.2 1.6 %collective-permute-start.17 = (f32[512,128]{1,0:T(8,128)S(1)}, f32[512,128]{1,0:T(8,128)S(1)}, u32[]{:S(2)}, u32[]{:S(2)}) collective-permute-start(f32[512,128]{1,0:T(8,128)S(1)} %get-tuple-element.66), channel_id=1, source_target_pairs={{0,2},{1,3},{2,0},{3,1},{4,6},{5,7},{6,4},{7,5},{8,10},{9,11},{10,... | collective-permute-start | bytes 786440 | tf_op jit(solution)/shard_map/ppermute | solution.py:453
  89.1 3.7 %grams.6 = (f32[512,128]{1,0:T(8,128)S(1)}, f32[512,128]{1,0:T(8,128)S(1)}) custom-call(bf16[1024,1024]{1,0:T(8,128)(2,1)S(1)} %get-tuple-element.53.refs_0_, bf16[1024,1024]{1,0:T(8,128)(2,1)S(1)} %get-tuple-element.54.refs_1_, bf16[1024,128]{1,0:T(8,128)(2,1)S(1)} %get-tuple-element.61.refs_2_, bf16[1024,1024]{1,0:T(8,128)(2,1)S(1)} %get-tuple-element.56.refs_4_.refs_3_, ...), custom_call_target="tpu_custom_call" | custom-call | flops 1073741824 | bytes 8912896 | tf_op jit(solution)/shard_map/grams/pallas_call | solution.py:245
  92.8 1.6 %collective-permute-start.14 = (f32[512,128]{1,0:T(8,128)S(1)}, f32[512,128]{1,0:T(8,128)S(1)}, u32[]{:S(2)}, u32[]{:S(2)}) collective-permute-start(f32[512,128]{1,0:T(8,128)S(1)} %get-tuple-element.63), channel_id=1, source_target_pairs={{0,2},{1,3},{2,0},{3,1},{4,6},{5,7},{6,4},{7,5},{8,10},{9,11},{10,... | collective-permute-start | bytes 786440 | tf_op jit(solution)/shard_map/ppermute | solution.py:453
  94.4 3.7 %grams.8 = (f32[512,256]{1,0:T(8,128)S(1)}, f32[512,256]{1,0:T(8,128)S(1)}) custom-call(bf16[1024,1024]{1,0:T(8,128)(2,1)S(1)} %get-tuple-element.53.refs_0_, bf16[1024,1024]{1,0:T(8,128)(2,1)S(1)} %get-tuple-element.54.refs_1_, bf16[1024,256]{1,0:T(8,128)(2,1)S(1)} %get-tuple-element.67.refs_2_, bf16[1024,1024]{1,0:T(8,128)(2,1)S(1)} %get-tuple-element.56.refs_4_.refs_3_, ...), custom_call_target="tpu_custom_call" | custom-call | flops 2147483648 | bytes 9437184 | tf_op jit(solution)/shard_map/grams/pallas_call | solution.py:245
  98.7 3.7 %grams.9 = (f32[512,256]{1,0:T(8,128)S(1)}, f32[512,256]{1,0:T(8,128)S(1)}) custom-call(bf16[1024,1024]{1,0:T(8,128)(2,1)S(1)} %get-tuple-element.53.refs_0_, bf16[1024,1024]{1,0:T(8,128)(2,1)S(1)} %get-tuple-element.54.refs_1_, bf16[1024,256]{1,0:T(8,128)(2,1)S(1)} %get-tuple-element.70.refs_2_, bf16[1024,1024]{1,0:T(8,128)(2,1)S(1)} %get-tuple-element.56.refs_4_.refs_3_, ...), custom_call_target="tpu_custom_call" | custom-call | flops 2147483648 | bytes 9437184 | tf_op jit(solution)/shard_map/grams/pallas_call | solution.py:245
  102.5 1.6 %collective-permute-start.23 = (f32[512,256]{1,0:T(8,128)S(1)}, f32[512,256]{1,0:T(8,128)S(1)}, u32[]{:S(2)}, u32[]{:S(2)}) collective-permute-start(f32[512,256]{1,0:T(8,128)S(1)} %get-tuple-element.72), channel_id=1, source_target_pairs={{0,2},{1,3},{2,0},{3,1},{4,6},{5,7},{6,4},{7,5},{8,10},{9,11},{10,... | collective-permute-start | bytes 1572872 | tf_op jit(solution)/shard_map/ppermute | solution.py:453
  104.1 5.0 %factor_first.1.in_ref = f32[256,512]{1,0:T(8,128)S(1)} custom-call(f32[768,128]{1,0:T(8,128)S(1)} %get-tuple-element.58.keep_ref, f32[768,128]{1,0:T(8,128)S(1)} %collective-permute-done.11.near_ref, f32[384,128]{1,0:T(8,128)S(1)} %collective-permute-done.12.far_ref), custom_call_target="tpu_custom_call" | custom-call | flops 10000000000 | bytes 1048576 | tf_op jit(solution)/shard_map/factor_first/pallas_call | solution.py:341
  109.1 2.7 %collective-permute-start.18 = (f32[256,128]{1,0:T(8,128)S(1)}, f32[256,128]{1,0:T(8,128)S(1)}, u32[]{:S(2)}, u32[]{:S(2)}) collective-permute-start(f32[256,128]{1,0:T(8,128)S(1)} %add.9), channel_id=1, source_target_pairs={{0,4},{1,5},{2,6},{3,7},{4,0},{5,1},{6,2},{7,3},{8,12},{9,13},{10,... | collective-permute-start | bytes 393224 | tf_op jit(solution)/shard_map/ppermute | solution.py:455
  112.2 9.6 %collective-permute-done.20.near_ref = f32[512,256]{1,0:T(8,128)S(1)} collective-permute-done((f32[512,256]{1,0:T(8,128)S(1)}, f32[512,256]{1,0:T(8,128)S(1)}, u32[]{:S(2)}, u32[]{:S(2)}) %collective-permute-start.20) | collective-permute-done | bytes 524320 | tf_op jit(solution)/shard_map/ppermute | solution.py:453
  121.8 1.7 %collective-permute-start.21 = (f32[256,256]{1,0:T(8,128)S(1)}, f32[256,256]{1,0:T(8,128)S(1)}, u32[]{:S(2)}, u32[]{:S(2)}) collective-permute-start(f32[256,256]{1,0:T(8,128)S(1)} %add.10), channel_id=1, source_target_pairs={{0,4},{1,5},{2,6},{3,7},{4,0},{5,1},{6,2},{7,3},{8,12},{9,13},{10,... | collective-permute-start | bytes 786440 | tf_op jit(solution)/shard_map/ppermute | solution.py:455
  123.5 6.8 %collective-permute-done.23.near_ref = f32[512,256]{1,0:T(8,128)S(1)} collective-permute-done((f32[512,256]{1,0:T(8,128)S(1)}, f32[512,256]{1,0:T(8,128)S(1)}, u32[]{:S(2)}, u32[]{:S(2)}) %collective-permute-start.23) | collective-permute-done | bytes 524320 | tf_op jit(solution)/shard_map/ppermute | solution.py:453
  130.3 1.0 collective-permute-start.24
  131.3 5.1 %factor_last.1 = (f32[256,1024]{1,0:T(8,128)}, f32[256,256]{1,0:T(8,128)S(1)}) custom-call(f32[256,512]{1,0:T(8,128)S(1)} %factor_first.1.in_ref), custom_call_target="tpu_custom_call" | custom-call | flops 10000000000 | bytes 1048576 | tf_op jit(solution)/shard_map/factor_last/pallas_call | solution.py:356
  136.4 11.8 %collective-permute-done.24.far_ref = f32[256,256]{1,0:T(8,128)S(1)} collective-permute-done((f32[256,256]{1,0:T(8,128)S(1)}, f32[256,256]{1,0:T(8,128)S(1)}, u32[]{:S(2)}, u32[]{:S(2)}) %collective-permute-start.24) | collective-permute-done | bytes 262176 | tf_op jit(solution)/shard_map/ppermute | solution.py:455
  148.2 1.1 couple.4.whole_ref
  149.3 1.1 couple.5.whole_ref
  150.4 1.0 couple.6.whole_ref
  151.5 1.0 couple.7
  (50 shorter events, 7.7 us)
Async XLA Ops:
  5.4 28.5 %collective-permute-start = (bf16[3,1024,256]{2,1,0:T(8,128)(2,1)}, bf16[3,1024,256]{2,1,0:T(8,128)(2,1)}, u32[]{:S(2)}, u32[]{:S(2)}) collective-permute-start(bf16[3,1024,256]{2,1,0:T(8,128)(2,1)} %mix.2.own_ref), channel_id=1, source_target_pairs={{0,8},{8,0},{16,24},{24,16},{1,9},{9,1},{17,25},{25,17},{2,10},{10... | collective-permute-start | bytes 4718600 | tf_op jit(solution)/shard_map/ppermute | solution.py:424
  8.6 2.1 %collective-permute-start.5 = (bf16[1,1024,256]{2,1,0:T(8,128)(2,1)}, bf16[1,1024,256]{2,1,0:T(8,128)(2,1)S(1)}, u32[]{:S(2)}, u32[]{:S(2)}) collective-permute-start(bf16[1,1024,256]{2,1,0:T(8,128)(2,1)} %mix.3.own_ref), channel_id=1, source_target_pairs={{0,8},{8,0},{16,24},{24,16},{1,9},{9,1},{17,25},{25,17},{2,10},{10... | collective-permute-start | bytes 1572872 | tf_op jit(solution)/shard_map/ppermute | solution.py:424
  10.7 0.8 copy-start.8
  14.9 10.0 %collective-permute-start.7 = (bf16[1024,128]{1,0:T(8,128)(2,1)}, bf16[1024,128]{1,0:T(8,128)(2,1)S(1)}, u32[]{:S(2)}, u32[]{:S(2)}) collective-permute-start(bf16[1024,128]{1,0:T(8,128)(2,1)} %get-tuple-element.43.own_ref), channel_id=1, source_target_pairs={{0,16},{8,24},{16,0},{24,8},{1,17},{9,25},{17,1},{25,9},{2,18},{10... | collective-permute-start | bytes 786440 | tf_op jit(solution)/shard_map/ppermute | solution.py:415
  17.5 12.7 %collective-permute-start.6 = (bf16[1024,128]{1,0:T(8,128)(2,1)}, bf16[1024,128]{1,0:T(8,128)(2,1)S(1)}, u32[]{:S(2)}, u32[]{:S(2)}) collective-permute-start(bf16[1024,128]{1,0:T(8,128)(2,1)} %get-tuple-element.42.own_ref), channel_id=1, source_target_pairs={{0,16},{8,24},{16,0},{24,8},{1,17},{9,25},{17,1},{25,9},{2,18},{10... | collective-permute-start | bytes 786440 | tf_op jit(solution)/shard_map/ppermute | solution.py:415
  24.9 1.0 copy-start.2
  30.2 1.0 copy-start.5
  31.9 8.0 %copy-start.6 = (s32[2048]{0:T(1024)S(1)}, s32[2048]{0:T(1024)}, u32[]{:S(2)}) copy-start(s32[2048]{0:T(1024)} %param.7) | copy-start | bytes 24580
  31.9 8.0 %copy-start.7 = (s32[2048,1]{0,1:T(1,128)S(1)}, s32[2048,1]{0,1:T(1,128)}, u32[]{:S(2)}) copy-start(s32[2048,1]{0,1:T(1,128)} %param.8) | copy-start | bytes 24580
  31.9 14.0 %collective-permute-start.10 = (bf16[1024,128]{1,0:T(8,128)(2,1)S(1)}, bf16[1024,128]{1,0:T(8,128)(2,1)S(1)}, u32[]{:S(2)}, u32[]{:S(2)}) collective-permute-start(bf16[1024,128]{1,0:T(8,128)(2,1)S(1)} %get-tuple-element.52.right_ref.refs_3_), channel_id=1, source_target_pairs={{0,1},{1,0},{2,3},{3,2},{4,5},{5,4},{6,7},{7,6},{8,9},{9,8},{10,11... | collective-permute-start | bytes 786440 | tf_op jit(solution)/shard_map/ppermute | solution.py:419
  33.6 12.3 %collective-permute-start.9 = (bf16[1024,128]{1,0:T(8,128)(2,1)S(1)}, bf16[1024,128]{1,0:T(8,128)(2,1)S(1)}, u32[]{:S(2)}, u32[]{:S(2)}) collective-permute-start(bf16[1024,128]{1,0:T(8,128)(2,1)S(1)} %get-tuple-element.51.left_ref.refs_2_), channel_id=1, source_target_pairs={{0,1},{1,0},{2,3},{3,2},{4,5},{5,4},{6,7},{7,6},{8,9},{9,8},{10,11... | collective-permute-start | bytes 786440 | tf_op jit(solution)/shard_map/ppermute | solution.py:419
  37.8 16.7 %collective-permute-start.4 = (bf16[1024,256]{1,0:T(8,128)(2,1)}, bf16[1024,256]{1,0:T(8,128)(2,1)S(1)}, u32[]{:S(2)}, u32[]{:S(2)}) collective-permute-start(bf16[1024,256]{1,0:T(8,128)(2,1)} %get-tuple-element.41.own_ref), channel_id=1, source_target_pairs={{0,16},{8,24},{16,0},{24,8},{1,17},{9,25},{17,1},{25,9},{2,18},{10... | collective-permute-start | bytes 1572872 | tf_op jit(solution)/shard_map/ppermute | solution.py:415
  39.6 24.5 %collective-permute-start.3 = (bf16[1024,256]{1,0:T(8,128)(2,1)}, bf16[1024,256]{1,0:T(8,128)(2,1)S(1)}, u32[]{:S(2)}, u32[]{:S(2)}) collective-permute-start(bf16[1024,256]{1,0:T(8,128)(2,1)} %get-tuple-element.40.own_ref), channel_id=1, source_target_pairs={{0,16},{8,24},{16,0},{24,8},{1,17},{9,25},{17,1},{25,9},{2,18},{10... | collective-permute-start | bytes 1572872 | tf_op jit(solution)/shard_map/ppermute | solution.py:415
  41.7 4.2 %collective-permute-start.8 = (f32[4,1024]{1,0:T(4,128)S(1)}, f32[4,1024]{1,0:T(4,128)S(1)}, u32[]{:S(2)}, u32[]{:S(2)}) collective-permute-start(f32[4,1024]{1,0:T(4,128)S(1)} %get-tuple-element.55), channel_id=1, source_target_pairs={{0,1},{1,0},{2,3},{3,2},{4,5},{5,4},{6,7},{7,6},{8,9},{9,8},{10,11... | collective-permute-start | bytes 49160 | tf_op jit(solution)/shard_map/ppermute | solution.py:435
  47.0 28.8 %collective-permute-start.1 = (bf16[1024,128]{1,0:T(8,128)(2,1)}, bf16[1024,128]{1,0:T(8,128)(2,1)S(1)}, u32[]{:S(2)}, u32[]{:S(2)}) collective-permute-start(bf16[1024,128]{1,0:T(8,128)(2,1)} %get-tuple-element.38.own_ref), channel_id=1, source_target_pairs={{0,16},{8,24},{16,0},{24,8},{1,17},{9,25},{17,1},{25,9},{2,18},{10... | collective-permute-start | bytes 786440 | tf_op jit(solution)/shard_map/ppermute | solution.py:415
  48.6 25.0 %collective-permute-start.2 = (bf16[1024,128]{1,0:T(8,128)(2,1)}, bf16[1024,128]{1,0:T(8,128)(2,1)S(1)}, u32[]{:S(2)}, u32[]{:S(2)}) collective-permute-start(bf16[1024,128]{1,0:T(8,128)(2,1)} %get-tuple-element.39.own_ref), channel_id=1, source_target_pairs={{0,16},{8,24},{16,0},{24,8},{1,17},{9,25},{17,1},{25,9},{2,18},{10... | collective-permute-start | bytes 786440 | tf_op jit(solution)/shard_map/ppermute | solution.py:415
  49.1 5.3 %copy-start.1 = (bf16[1024,256]{1,0:T(8,128)(2,1)S(1)}, bf16[1024,256]{1,0:T(8,128)(2,1)}, u32[]{:S(2)}) copy-start(bf16[1024,256]{1,0:T(8,128)(2,1)} %get-tuple-element.41.own_ref) | copy-start | bytes 1572868
  52.9 11.2 %copy-start = (bf16[1024,256]{1,0:T(8,128)(2,1)S(1)}, bf16[1024,256]{1,0:T(8,128)(2,1)}, u32[]{:S(2)}) copy-start(bf16[1024,256]{1,0:T(8,128)(2,1)} %get-tuple-element.40.own_ref) | copy-start | bytes 1572868
  52.9 25.7 %collective-permute-start.11 = (f32[768,128]{1,0:T(8,128)S(1)}, f32[768,128]{1,0:T(8,128)S(1)}, u32[]{:S(2)}, u32[]{:S(2)}) collective-permute-start(f32[768,128]{1,0:T(8,128)S(1)} %get-tuple-element.59), channel_id=1, source_target_pairs={{0,2},{1,3},{2,0},{3,1},{4,6},{5,7},{6,4},{7,5},{8,10},{9,11},{10,... | collective-permute-start | bytes 1179656 | tf_op jit(solution)/shard_map/ppermute | solution.py:453
  55.4 18.2 %copy-start.4 = (bf16[1024,128]{1,0:T(8,128)(2,1)S(1)}, bf16[1024,128]{1,0:T(8,128)(2,1)}, u32[]{:S(2)}) copy-start(bf16[1024,128]{1,0:T(8,128)(2,1)} %get-tuple-element.39.own_ref) | copy-start | bytes 786436
  65.0 10.8 %copy-start.3 = (bf16[1024,128]{1,0:T(8,128)(2,1)S(1)}, bf16[1024,128]{1,0:T(8,128)(2,1)}, u32[]{:S(2)}) copy-start(bf16[1024,128]{1,0:T(8,128)(2,1)} %get-tuple-element.38.own_ref) | copy-start | bytes 786436
  65.0 29.5 %collective-permute-start.19 = (bf16[1024,256]{1,0:T(8,128)(2,1)S(1)}, bf16[1024,256]{1,0:T(8,128)(2,1)S(1)}, u32[]{:S(2)}, u32[]{:S(2)}) collective-permute-start(bf16[1024,256]{1,0:T(8,128)(2,1)S(1)} %get-tuple-element.67.refs_2_), channel_id=1, source_target_pairs={{0,1},{1,0},{2,3},{3,2},{4,5},{5,4},{6,7},{7,6},{8,9},{9,8},{10,11... | collective-permute-start | bytes 1572872 | tf_op jit(solution)/shard_map/ppermute | solution.py:419
  74.4 9.2 %collective-permute-start.16 = (bf16[1024,128]{1,0:T(8,128)(2,1)S(1)}, bf16[1024,128]{1,0:T(8,128)(2,1)S(1)}, u32[]{:S(2)}, u32[]{:S(2)}) collective-permute-start(bf16[1024,128]{1,0:T(8,128)(2,1)S(1)} %get-tuple-element.64.refs_2_), channel_id=1, source_target_pairs={{0,1},{1,0},{2,3},{3,2},{4,5},{5,4},{6,7},{7,6},{8,9},{9,8},{10,11... | collective-permute-start | bytes 786440 | tf_op jit(solution)/shard_map/ppermute | solution.py:419
  76.6 12.6 %collective-permute-start.13 = (bf16[1024,128]{1,0:T(8,128)(2,1)S(1)}, bf16[1024,128]{1,0:T(8,128)(2,1)S(1)}, u32[]{:S(2)}, u32[]{:S(2)}) collective-permute-start(bf16[1024,128]{1,0:T(8,128)(2,1)S(1)} %get-tuple-element.61.refs_2_), channel_id=1, source_target_pairs={{0,1},{1,0},{2,3},{3,2},{4,5},{5,4},{6,7},{7,6},{8,9},{9,8},{10,11... | collective-permute-start | bytes 786440 | tf_op jit(solution)/shard_map/ppermute | solution.py:419
  77.2 21.6 %collective-permute-start.22 = (bf16[1024,256]{1,0:T(8,128)(2,1)S(1)}, bf16[1024,256]{1,0:T(8,128)(2,1)S(1)}, u32[]{:S(2)}, u32[]{:S(2)}) collective-permute-start(bf16[1024,256]{1,0:T(8,128)(2,1)S(1)} %get-tuple-element.70.refs_2_), channel_id=1, source_target_pairs={{0,1},{1,0},{2,3},{3,2},{4,5},{5,4},{6,7},{7,6},{8,9},{9,8},{10,11... | collective-permute-start | bytes 1572872 | tf_op jit(solution)/shard_map/ppermute | solution.py:419
  78.6 25.5 %collective-permute-start.12 = (f32[384,128]{1,0:T(8,128)S(1)}, f32[384,128]{1,0:T(8,128)S(1)}, u32[]{:S(2)}, u32[]{:S(2)}) collective-permute-start(f32[384,128]{1,0:T(8,128)S(1)} %add.7), channel_id=1, source_target_pairs={{0,4},{1,5},{2,6},{3,7},{4,0},{5,1},{6,2},{7,3},{8,12},{9,13},{10,... | collective-permute-start | bytes 589832 | tf_op jit(solution)/shard_map/ppermute | solution.py:455
  87.2 21.9 %collective-permute-start.17 = (f32[512,128]{1,0:T(8,128)S(1)}, f32[512,128]{1,0:T(8,128)S(1)}, u32[]{:S(2)}, u32[]{:S(2)}) collective-permute-start(f32[512,128]{1,0:T(8,128)S(1)} %get-tuple-element.66), channel_id=1, source_target_pairs={{0,2},{1,3},{2,0},{3,1},{4,6},{5,7},{6,4},{7,5},{8,10},{9,11},{10,... | collective-permute-start | bytes 786440 | tf_op jit(solution)/shard_map/ppermute | solution.py:453
  92.8 18.9 %collective-permute-start.14 = (f32[512,128]{1,0:T(8,128)S(1)}, f32[512,128]{1,0:T(8,128)S(1)}, u32[]{:S(2)}, u32[]{:S(2)}) collective-permute-start(f32[512,128]{1,0:T(8,128)S(1)} %get-tuple-element.63), channel_id=1, source_target_pairs={{0,2},{1,3},{2,0},{3,1},{4,6},{5,7},{6,4},{7,5},{8,10},{9,11},{10,... | collective-permute-start | bytes 786440 | tf_op jit(solution)/shard_map/ppermute | solution.py:453
  98.2 23.6 %collective-permute-start.20 = (f32[512,256]{1,0:T(8,128)S(1)}, f32[512,256]{1,0:T(8,128)S(1)}, u32[]{:S(2)}, u32[]{:S(2)}) collective-permute-start(f32[512,256]{1,0:T(8,128)S(1)} %get-tuple-element.69), channel_id=1, source_target_pairs={{0,2},{1,3},{2,0},{3,1},{4,6},{5,7},{6,4},{7,5},{8,10},{9,11},{10,... | collective-permute-start | bytes 1572872 | tf_op jit(solution)/shard_map/ppermute | solution.py:453
  102.5 27.8 %collective-permute-start.23 = (f32[512,256]{1,0:T(8,128)S(1)}, f32[512,256]{1,0:T(8,128)S(1)}, u32[]{:S(2)}, u32[]{:S(2)}) collective-permute-start(f32[512,256]{1,0:T(8,128)S(1)} %get-tuple-element.72), channel_id=1, source_target_pairs={{0,2},{1,3},{2,0},{3,1},{4,6},{5,7},{6,4},{7,5},{8,10},{9,11},{10,... | collective-permute-start | bytes 1572872 | tf_op jit(solution)/shard_map/ppermute | solution.py:453
  109.1 41.3 %collective-permute-start.18 = (f32[256,128]{1,0:T(8,128)S(1)}, f32[256,128]{1,0:T(8,128)S(1)}, u32[]{:S(2)}, u32[]{:S(2)}) collective-permute-start(f32[256,128]{1,0:T(8,128)S(1)} %add.9), channel_id=1, source_target_pairs={{0,4},{1,5},{2,6},{3,7},{4,0},{5,1},{6,2},{7,3},{8,12},{9,13},{10,... | collective-permute-start | bytes 393224 | tf_op jit(solution)/shard_map/ppermute | solution.py:455
  111.8 39.7 %collective-permute-start.15 = (f32[256,128]{1,0:T(8,128)S(1)}, f32[256,128]{1,0:T(8,128)S(1)}, u32[]{:S(2)}, u32[]{:S(2)}) collective-permute-start(f32[256,128]{1,0:T(8,128)S(1)} %add.8), channel_id=1, source_target_pairs={{0,4},{1,5},{2,6},{3,7},{4,0},{5,1},{6,2},{7,3},{8,12},{9,13},{10,... | collective-permute-start | bytes 393224 | tf_op jit(solution)/shard_map/ppermute | solution.py:455
  121.8 27.5 %collective-permute-start.21 = (f32[256,256]{1,0:T(8,128)S(1)}, f32[256,256]{1,0:T(8,128)S(1)}, u32[]{:S(2)}, u32[]{:S(2)}) collective-permute-start(f32[256,256]{1,0:T(8,128)S(1)} %add.10), channel_id=1, source_target_pairs={{0,4},{1,5},{2,6},{3,7},{4,0},{5,1},{6,2},{7,3},{8,12},{9,13},{10,... | collective-permute-start | bytes 786440 | tf_op jit(solution)/shard_map/ppermute | solution.py:455
  130.3 17.9 %collective-permute-start.24 = (f32[256,256]{1,0:T(8,128)S(1)}, f32[256,256]{1,0:T(8,128)S(1)}, u32[]{:S(2)}, u32[]{:S(2)}) collective-permute-start(f32[256,256]{1,0:T(8,128)S(1)} %add.11), channel_id=1, source_target_pairs={{0,4},{1,5},{2,6},{3,7},{4,0},{5,1},{6,2},{7,3},{8,12},{9,13},{10,... | collective-permute-start | bytes 786440 | tf_op jit(solution)/shard_map/ppermute | solution.py:455
